TPU v7x, 32 devices: a whole 2x2x4 slice. The times are simulated.
32 devices in a mesh: expert: 16 (over z, y, core), dp: 2 (over x).
Axes of the slice: x: 2, y: 2, z: 4, core: 2. Of those that a mesh axis runs over, the one named last changes fastest.
Arguments:
- tokens: bfloat16 [2, 2048, 1024], P(None, ('expert', 'dp')), may hold values from -6 to 6
- routes: int32 [2, 2048, 6], P(None, ('expert', 'dp')), may hold values from 0 to 15, all different within a row; in each aligned block of 64 rows (0 to 63, 64 to 127, ..., all dimensions but the last counted through in order) at most 32 rows name the same one
- gate_weights: float32 [2, 2048, 6], P(None, ('expert', 'dp')), may hold values from 0.05 to 0.35
- cotangent: bfloat16 [2, 2048, 1024], P(None, ('expert', 'dp')), may hold values from -6 to 6
- expert_plan: int32 [16], replicated, may hold values from 0 to 15, each once
- weight_in: bfloat16 [16, 1024, 1536], P('expert', 'dp'), may hold values from -0.1875 to 0.1875
- weight_out: bfloat16 [16, 768, 1024], P('expert', 'dp'), may hold values from -0.21875 to 0.21875
- first_in: float32 [16, 1024, 1536], P('expert', 'dp'), may hold values from -6 to 6
- second_in: float32 [16, 1024, 1536], P('expert', 'dp'), may hold values from 0.5 to 20
- first_out: float32 [16, 768, 1024], P('expert', 'dp'), may hold values from -6 to 6
- second_out: float32 [16, 768, 1024], P('expert', 'dp'), may hold values from 0.5 to 20
Outputs:
- layer_output: bfloat16 [2, 2048, 1024], P(None, ('expert', 'dp'))
- token_gradient: bfloat16 [2, 2048, 1024], P(None, ('expert', 'dp'))
- weight_in_next: bfloat16 [16, 1024, 1536], P('expert', 'dp')
- weight_out_next: bfloat16 [16, 768, 1024], P('expert', 'dp')
- first_in_next: float32 [16, 1024, 1536], P('expert', 'dp')
- second_in_next: float32 [16, 1024, 1536], P('expert', 'dp')
- first_out_next: float32 [16, 768, 1024], P('expert', 'dp')
- second_out_next: float32 [16, 768, 1024], P('expert', 'dp')
Inputs may be any that keep to these rules, and one draw needn't show every extreme that they name: `routes`: each row names 6 different experts. In the 64 rows of one device in one micro-batch (an aligned block), no expert is named by more than 32 rows; in some blocks one expert is named by exactly 32 rows. A permutation. Before the migration, index d of the expert axis holds expert d; after it, expert expert_plan[d].
All inputs are finite; a program needn't handle non-finite values.
Results may differ from a plain program's by a relative error of at most 0.014.
Values may be sent and summed in bfloat16 or wider, within the bound.
A program may use at most 128 MiB of HBM per device.

v0:
```python
import jax
import jax.numpy as jnp
from jax import lax
from jax.sharding import PartitionSpec as P

beta_one = 0.9
beta_two = 0.95
learn_rate = 0.00042
decay_rate = 0.1
epsilon = 1e-08
steps_done = 10


def as_sent(x):
    return jax.tree.map(lambda a: a.astype(jnp.bfloat16) if a.dtype == jnp.float32 else a, x)


def adam_update(weight, gradient, first, second):
    first_new = beta_one * first + (1.0 - beta_one) * gradient
    second_new = beta_two * second + (1.0 - beta_two) * gradient * gradient
    ratio = (
        first_new
        / (1.0 - beta_one**steps_done)
        / (jnp.sqrt(second_new / (1.0 - beta_two**steps_done)) + epsilon)
    )
    master = weight.astype(jnp.float32)
    return (
        (master - learn_rate * (ratio + decay_rate * master)).astype(jnp.bfloat16),
        first_new,
        second_new,
    )


def relocate_weights(pair, expert_plan):
    count = expert_plan.shape[0]
    spread = (
        lax.all_to_all(
            pair[0].reshape(count, -1), "expert", split_axis=0, concat_axis=0, tiled=True
        ),
        lax.all_to_all(
            pair[1].reshape(count, -1), "expert", split_axis=0, concat_axis=0, tiled=True
        ),
    )
    picked_first = jnp.take(spread[0], expert_plan, axis=0)
    picked_second = jnp.take(spread[1], expert_plan, axis=0)
    landed = (
        lax.all_to_all(picked_first, "expert", split_axis=0, concat_axis=0, tiled=True),
        lax.all_to_all(picked_second, "expert", split_axis=0, concat_axis=0, tiled=True),
    )
    return (landed[0].reshape(pair[0].shape), landed[1].reshape(pair[1].shape))


def relocate_moments(group, expert_plan):
    count = expert_plan.shape[0]
    spread = (
        lax.all_to_all(
            group[0].reshape(count, -1).astype(jnp.bfloat16),
            "expert",
            split_axis=0,
            concat_axis=0,
            tiled=True,
        ).astype(jnp.float32),
        lax.all_to_all(
            group[1].reshape(count, -1).astype(jnp.bfloat16),
            "expert",
            split_axis=0,
            concat_axis=0,
            tiled=True,
        ).astype(jnp.float32),
        lax.all_to_all(
            group[2].reshape(count, -1).astype(jnp.bfloat16),
            "expert",
            split_axis=0,
            concat_axis=0,
            tiled=True,
        ).astype(jnp.float32),
        lax.all_to_all(
            group[3].reshape(count, -1).astype(jnp.bfloat16),
            "expert",
            split_axis=0,
            concat_axis=0,
            tiled=True,
        ).astype(jnp.float32),
    )
    picked = [jnp.take(member, expert_plan, axis=0) for member in spread]
    landed = (
        lax.all_to_all(as_sent(picked[0]), "expert", split_axis=0, concat_axis=0, tiled=True),
        lax.all_to_all(as_sent(picked[1]), "expert", split_axis=0, concat_axis=0, tiled=True),
        lax.all_to_all(as_sent(picked[2]), "expert", split_axis=0, concat_axis=0, tiled=True),
        lax.all_to_all(as_sent(picked[3]), "expert", split_axis=0, concat_axis=0, tiled=True),
    )
    return tuple((landed[place].reshape(group[place].shape) for place in range(4)))


def slot_layout(chosen, holders, capacity):
    count = holders.shape[0]
    hits = (chosen[:, :, None] == holders[None, None, :]).astype(jnp.int32)
    per_token = jnp.sum(hits, axis=1)
    before = jnp.cumsum(per_token, axis=0) - per_token
    ranks = jnp.sum(hits * before[:, None, :], axis=2)
    owners = jnp.sum(hits * jnp.arange(count, dtype=jnp.int32)[None, None, :], axis=2)
    return owners * capacity + ranks


def expert_forward(rows, weight_first, weight_second):
    hidden_width = weight_second.shape[0]
    pre = jnp.dot(rows, weight_first, preferred_element_type=jnp.float32)
    gate_part = pre[:, :hidden_width]
    up_part = pre[:, hidden_width:]
    sigma = jax.nn.sigmoid(gate_part)
    hidden = (gate_part * sigma * up_part).astype(jnp.bfloat16)
    output = jnp.dot(hidden, weight_second, preferred_element_type=jnp.float32).astype(jnp.bfloat16)
    return (output, gate_part, up_part, sigma, hidden)


def on_device(
    tokens,
    routes,
    gate_weights,
    cotangent,
    expert_plan,
    weight_in,
    weight_out,
    first_in,
    second_in,
    first_out,
    second_out,
):
    count = lax.axis_size("expert")
    micro_count = tokens.shape[0]
    token_count = tokens.shape[1]
    width = tokens.shape[2]
    top_count = routes.shape[2]
    capacity = token_count * top_count * 4 // (3 * count)
    total_slots = count * capacity
    weight_in, weight_out = relocate_weights((weight_in, weight_out), expert_plan)
    first_in, second_in, first_out, second_out = relocate_moments(
        (first_in, second_in, first_out, second_out), expert_plan
    )
    whole_in, whole_out = (
        lax.all_gather(weight_in[0], "dp", axis=0, tiled=True),
        lax.all_gather(weight_out[0], "dp", axis=0, tiled=True),
    )
    hidden_width = whole_out.shape[0]
    grad_in = jnp.zeros((width, 2 * hidden_width), jnp.float32)
    grad_out = jnp.zeros((hidden_width, width), jnp.float32)
    blank = jnp.zeros((1, width), jnp.bfloat16)
    layer_parts = []
    token_parts = []
    for micro in range(micro_count):
        slots = slot_layout(routes[micro], expert_plan, capacity)
        flat_slots = slots.reshape(-1)
        marks = (flat_slots[:, None] == jnp.arange(total_slots, dtype=jnp.int32)[None, :]).astype(
            jnp.int32
        )
        pair_ids = jnp.arange(flat_slots.shape[0], dtype=jnp.int32) + 1
        anchor = jnp.sum(marks * pair_ids[:, None], axis=0)
        token_anchor = jnp.where(anchor > 0, (anchor - 1) // top_count + 1, 0)
        outgoing = jnp.take(jnp.concatenate([blank, tokens[micro]], axis=0), token_anchor, axis=0)
        arrived = lax.all_to_all(
            outgoing.reshape(count, capacity, width),
            "expert",
            split_axis=0,
            concat_axis=0,
            tiled=True,
        ).reshape(total_slots, width)
        output, gate_part, up_part, sigma, hidden = expert_forward(arrived, whole_in, whole_out)
        returned = lax.all_to_all(
            output.reshape(count, capacity, width),
            "expert",
            split_axis=0,
            concat_axis=0,
            tiled=True,
        ).reshape(total_slots, width)
        picked = jnp.take(returned, flat_slots, axis=0).reshape(token_count, top_count, width)
        gates = gate_weights[micro]
        layer_parts.append(
            jnp.sum(gates[:, :, None] * picked.astype(jnp.float32), axis=1).astype(jnp.bfloat16)
        )
        scaled = (gates[:, :, None] * cotangent[micro][:, None, :].astype(jnp.float32)).astype(
            jnp.bfloat16
        )
        outgoing_grad = jnp.take(
            jnp.concatenate([blank, scaled.reshape(-1, width)], axis=0), anchor, axis=0
        )
        arrived_grad = lax.all_to_all(
            outgoing_grad.reshape(count, capacity, width),
            "expert",
            split_axis=0,
            concat_axis=0,
            tiled=True,
        ).reshape(total_slots, width)
        hidden_grad = lax.dot_general(
            arrived_grad, whole_out, (((1,), (1,)), ((), ())), preferred_element_type=jnp.float32
        )
        pre_grad = jnp.concatenate(
            [
                hidden_grad * up_part * sigma * (1.0 + gate_part * (1.0 - sigma)),
                hidden_grad * gate_part * sigma,
            ],
            axis=1,
        ).astype(jnp.bfloat16)
        grad_in = grad_in + lax.dot_general(
            arrived, pre_grad, (((0,), (0,)), ((), ())), preferred_element_type=jnp.float32
        )
        grad_out = grad_out + lax.dot_general(
            hidden, arrived_grad, (((0,), (0,)), ((), ())), preferred_element_type=jnp.float32
        )
        token_part = lax.dot_general(
            pre_grad, whole_in, (((1,), (1,)), ((), ())), preferred_element_type=jnp.float32
        ).astype(jnp.bfloat16)
        returned_grad = lax.all_to_all(
            token_part.reshape(count, capacity, width),
            "expert",
            split_axis=0,
            concat_axis=0,
            tiled=True,
        ).reshape(total_slots, width)
        picked_grad = jnp.take(returned_grad, flat_slots, axis=0).reshape(
            token_count, top_count, width
        )
        token_parts.append(jnp.sum(picked_grad.astype(jnp.float32), axis=1).astype(jnp.bfloat16))
    share_in, share_out = (
        lax.psum_scatter(
            grad_in.astype(jnp.bfloat16), "dp", scatter_dimension=0, tiled=True
        ).astype(jnp.float32),
        lax.psum_scatter(
            grad_out.astype(jnp.bfloat16), "dp", scatter_dimension=0, tiled=True
        ).astype(jnp.float32),
    )
    new_in, first_in_new, second_in_new = adam_update(
        weight_in, share_in[None], first_in, second_in
    )
    new_out, first_out_new, second_out_new = adam_update(
        weight_out, share_out[None], first_out, second_out
    )
    return (
        jnp.stack(layer_parts, axis=0),
        jnp.stack(token_parts, axis=0),
        new_in,
        new_out,
        first_in_new,
        second_in_new,
        first_out_new,
        second_out_new,
    )


def solution(mesh):
    placed = (
        P(None, ("expert", "dp"), None),
        P(None, ("expert", "dp"), None),
        P(None, ("expert", "dp"), None),
        P(None, ("expert", "dp"), None),
        P(),
        P("expert", "dp", None),
        P("expert", "dp", None),
        P("expert", "dp", None),
        P("expert", "dp", None),
        P("expert", "dp", None),
        P("expert", "dp", None),
    )
    return jax.shard_map(
        on_device,
        mesh=mesh,
        in_specs=placed,
        out_specs=(
            P(None, ("expert", "dp"), None),
            P(None, ("expert", "dp"), None),
            P("expert", "dp", None),
            P("expert", "dp", None),
            P("expert", "dp", None),
            P("expert", "dp", None),
            P("expert", "dp", None),
            P("expert", "dp", None),
        ),
        check_vma=False,
    )
```

profile of v0, /device:TPU:0, one launch (start us, length us, event | category | flops | bytes accessed | tf_op | source)
XLA Modules:
  0.0 793.0 jit_solution(807611301252723767)
XLA Ops:
  34.0 11.0 %all-to-all-done.3 = bf16[16,2,12288]{2,1,0:T(2,128)(2,1)S(1)} async-done(((bf16[16,2,12288]{2,1,0:T(2,128)(2,1)}), bf16[16,2,12288]{2,1,0:T(2,128)(2,1)S(1)}, u32[]{:S(2)}, u32[]{:S(2)}) %all-to-all-start.3) | async-done | bytes 786464 | tf_op jit(solution)/shard_map/all_to_all | solution.py:40
  60.0 10.5 %all-to-all-done.16 = bf16[16,2,12288]{2,1,0:T(2,128)(2,1)S(1)} async-done(((bf16[16,2,12288]{2,1,0:T(2,128)(2,1)}), bf16[16,2,12288]{2,1,0:T(2,128)(2,1)S(1)}, u32[]{:S(2)}, u32[]{:S(2)}) %all-to-all-start.16) | async-done | bytes 786464 | tf_op jit(solution)/shard_map/all_to_all | solution.py:70
  82.1 12.5 %all-to-all-done.18 = bf16[16,2,12288]{2,1,0:T(2,128)(2,1)S(1)} async-done(((bf16[16,2,12288]{2,1,0:T(2,128)(2,1)}), bf16[16,2,12288]{2,1,0:T(2,128)(2,1)S(1)}, u32[]{:S(2)}, u32[]{:S(2)}) %all-to-all-start.18) | async-done | bytes 786464 | tf_op jit(solution)/shard_map/all_to_all | solution.py:77
  108.0 14.9 %all-to-all-done.6 = bf16[16,32,1024]{2,1,0:T(8,128)(2,1)S(1)} async-done(((bf16[16,32,1024]{2,1,0:T(8,128)(2,1)}), bf16[16,32,1024]{2,1,0:T(8,128)(2,1)S(1)}, u32[]{:S(2)}, u32[]{:S(2)}) %all-to-all-start.6) | async-done | bytes 1048608 | tf_op jit(solution)/shard_map/all_to_all | solution.py:160
  134.8 17.7 %all-to-all-done.10 = bf16[16,32,1024]{2,1,0:T(8,128)(2,1)S(1)} async-done(((bf16[16,32,1024]{2,1,0:T(8,128)(2,1)}), bf16[16,32,1024]{2,1,0:T(8,128)(2,1)S(1)}, u32[]{:S(2)}, u32[]{:S(2)}) %all-to-all-start.10) | async-done | bytes 1048608 | tf_op jit(solution)/shard_map/all_to_all | solution.py:186
  166.9 15.5 %all-to-all-done = bf16[16,32,1024]{2,1,0:T(8,128)(2,1)S(1)} async-done(((bf16[16,32,1024]{2,1,0:T(8,128)(2,1)}), bf16[16,32,1024]{2,1,0:T(8,128)(2,1)S(1)}, u32[]{:S(2)}, u32[]{:S(2)}) %all-to-all-start) | async-done | bytes 1048608 | tf_op jit(solution)/shard_map/all_to_all | solution.py:160
  194.5 11.3 %reduce.12 = bf16[16,49152]{1,0:T(8,128)(2,1)} reduce(bf16[16,1,49152]{2,1,0:T(2,128)(2,1)S(1)} %all_to_all.116, bf16[]{:T(256)} %broadcast.308), dimensions={1}, to_apply=%all_to_all.116.reduce_sub_computation | reduce | bytes 3145730 | tf_op jit(solution)/shard_map/all_to_all | solution.py:37
  222.7 29.0 %all-to-all-done.1 = bf16[16,2,24576]{2,1,0:T(2,128)(2,1)S(1)} async-done(((bf16[16,2,24576]{2,1,0:T(2,128)(2,1)}), bf16[16,2,24576]{2,1,0:T(2,128)(2,1)S(1)}, u32[]{:S(2)}, u32[]{:S(2)}) %all-to-all-start.1) | async-done | bytes 1572896 | tf_op jit(solution)/shard_map/all_to_all | solution.py:37
  251.8 9.2 %all-to-all-start.4 = ((bf16[16,2,12288]{2,1,0:T(2,128)(2,1)}), bf16[16,2,12288]{2,1,0:T(2,128)(2,1)}, u32[]{:S(2)}, u32[]{:S(2)}) async-start(bf16[16,2,12288]{2,1,0:T(2,128)(2,1)} %reshape.606), calls=%async_computation.4 | async-start | bytes 1572864 | tf_op jit(solution)/shard_map/all_to_all | solution.py:48
  268.4 11.3 %reduce.16 = bf16[16,49152]{1,0:T(8,128)(2,1)} reduce(bf16[16,1,49152]{2,1,0:T(2,128)(2,1)S(1)} %convert_element_type.320, bf16[]{:T(256)} %broadcast.308), dimensions={1}, to_apply=%convert_element_type.320.reduce_sub_computation | reduce | bytes 3145730 | tf_op jit(solution)/shard_map/convert_element_type | solution.py:57
  295.1 11.3 %reduce.17 = bf16[16,49152]{1,0:T(8,128)(2,1)} reduce(bf16[16,1,49152]{2,1,0:T(2,128)(2,1)S(1)} %convert_element_type.321, bf16[]{:T(256)} %broadcast.308), dimensions={1}, to_apply=%convert_element_type.321.reduce_sub_computation | reduce | bytes 3145730 | tf_op jit(solution)/shard_map/convert_element_type | solution.py:64
  343.0 25.1 %all-to-all-done.14 = bf16[16,2,24576]{2,1,0:T(2,128)(2,1)S(1)} async-done(((bf16[16,2,24576]{2,1,0:T(2,128)(2,1)}), bf16[16,2,24576]{2,1,0:T(2,128)(2,1)S(1)}, u32[]{:S(2)}, u32[]{:S(2)}) %all-to-all-start.14) | async-done | bytes 1572896 | tf_op jit(solution)/shard_map/all_to_all | solution.py:63
  385.6 23.4 %all-to-all-done.2 = bf16[16,2,24576]{2,1,0:T(2,128)(2,1)S(1)} async-done(((bf16[16,2,24576]{2,1,0:T(2,128)(2,1)}), bf16[16,2,24576]{2,1,0:T(2,128)(2,1)S(1)}, u32[]{:S(2)}, u32[]{:S(2)}) %all-to-all-start.2) | async-done | bytes 1572896 | tf_op jit(solution)/shard_map/all_to_all | solution.py:47
  409.0 9.2 %all-to-all-start.19 = ((bf16[16,2,12288]{2,1,0:T(2,128)(2,1)}), bf16[16,2,12288]{2,1,0:T(2,128)(2,1)}, u32[]{:S(2)}, u32[]{:S(2)}) async-start(bf16[16,2,12288]{2,1,0:T(2,128)(2,1)} %reshape.618), calls=%async_computation.21 | async-start | bytes 1572864 | tf_op jit(solution)/shard_map/all_to_all | solution.py:90
  423.8 10.0 %reshape.613 = bf16[16,1,49152]{2,1,0:T(2,128)(2,1)} reshape(bf16[16,2,24576]{2,1,0:T(2,128)(2,1)} %all-to-all-done.12) | data formatting | bytes 3145728
  461.0 10.7 %reduce.2 = bf16[16,49152]{1,0:T(8,128)(2,1)} reduce(bf16[16,1,49152]{2,1,0:T(2,128)(2,1)S(1)} %reshape.603, bf16[]{:T(256)} %constant.159), dimensions={1}, to_apply=%all_to_all.92.reduce_sub_computation | reduce | bytes 3145730 | tf_op jit(solution)/shard_map/all_to_all | solution.py:47
  488.2 11.4 %all-to-all-done.17 = bf16[16,2,12288]{2,1,0:T(2,128)(2,1)} async-done(((bf16[16,2,12288]{2,1,0:T(2,128)(2,1)}), bf16[16,2,12288]{2,1,0:T(2,128)(2,1)}, u32[]{:S(2)}, u32[]{:S(2)}) %all-to-all-start.17) | async-done | bytes 786464 | tf_op jit(solution)/shard_map/all_to_all | solution.py:89
  522.9 14.0 %all-to-all-done.15 = bf16[16,2,24576]{2,1,0:T(2,128)(2,1)S(1)} async-done(((bf16[16,2,24576]{2,1,0:T(2,128)(2,1)}), bf16[16,2,24576]{2,1,0:T(2,128)(2,1)S(1)}, u32[]{:S(2)}, u32[]{:S(2)}) %all-to-all-start.15) | async-done | bytes 1572896 | tf_op jit(solution)/shard_map/all_to_all | solution.py:88
  592.8 19.3 %all-to-all-done.11 = bf16[16,32,1024]{2,1,0:T(8,128)(2,1)S(1)} async-done(((bf16[16,32,1024]{2,1,0:T(8,128)(2,1)}), bf16[16,32,1024]{2,1,0:T(8,128)(2,1)S(1)}, u32[]{:S(2)}, u32[]{:S(2)}) %all-to-all-start.11) | async-done | bytes 1048608 | tf_op jit(solution)/shard_map/all_to_all | solution.py:212
  632.6 9.2 %all-to-all-done.7 = bf16[16,32,1024]{2,1,0:T(8,128)(2,1)S(1)} async-done(((bf16[16,32,1024]{2,1,0:T(8,128)(2,1)}), bf16[16,32,1024]{2,1,0:T(8,128)(2,1)S(1)}, u32[]{:S(2)}, u32[]{:S(2)}) %all-to-all-start.7) | async-done | bytes 1048608 | tf_op jit(solution)/shard_map/all_to_all | solution.py:168
  688.9 10.0 %reshape.611 = bf16[16,1,49152]{2,1,0:T(2,128)(2,1)} reshape(bf16[16,2,24576]{2,1,0:T(2,128)(2,1)} %copy-done.3) | data formatting | bytes 3145728
  698.9 12.7 %convert_reduce_fusion = f32[16,49152]{1,0:T(8,128)} fusion(bf16[16,1,49152]{2,1,0:T(2,128)(2,1)} %reshape.611), kind=kLoop, calls=%fused_computation.26 | loop fusion | flops 1572864 | bytes 4718592 | tf_op jit(solution)/shard_map/convert_element_type | solution.py:20
  715.0 10.2 %reshape.615 = bf16[16,1,49152]{2,1,0:T(2,128)(2,1)} reshape(bf16[16,2,24576]{2,1,0:T(2,128)(2,1)} %copy-done.4) | data formatting | bytes 3145728
  725.1 12.7 %convert_reduce_fusion.1 = f32[16,49152]{1,0:T(8,128)} fusion(bf16[16,1,49152]{2,1,0:T(2,128)(2,1)} %reshape.615), kind=kLoop, calls=%fused_computation.27 | loop fusion | flops 1572864 | bytes 4718592 | tf_op jit(solution)/shard_map/convert_element_type | solution.py:19
  (306 shorter events, 445.9 us)
Async XLA Ops:
  18.7 26.4 %all-to-all-start.3 = ((bf16[16,2,12288]{2,1,0:T(2,128)(2,1)}), bf16[16,2,12288]{2,1,0:T(2,128)(2,1)S(1)}, u32[]{:S(2)}, u32[]{:S(2)}) async-start(bf16[16,2,12288]{2,1,0:T(2,128)(2,1)} %reshape.604), calls=%async_computation.3 | async-start | bytes 1572864 | tf_op jit(solution)/shard_map/all_to_all | solution.py:40
  45.9 24.6 %all-to-all-start.16 = ((bf16[16,2,12288]{2,1,0:T(2,128)(2,1)}), bf16[16,2,12288]{2,1,0:T(2,128)(2,1)S(1)}, u32[]{:S(2)}, u32[]{:S(2)}) async-start(bf16[16,2,12288]{2,1,0:T(2,128)(2,1)} %reshape.620), calls=%async_computation.17 | async-start | bytes 1572864 | tf_op jit(solution)/shard_map/all_to_all | solution.py:70
  70.5 24.1 %all-to-all-start.18 = ((bf16[16,2,12288]{2,1,0:T(2,128)(2,1)}), bf16[16,2,12288]{2,1,0:T(2,128)(2,1)S(1)}, u32[]{:S(2)}, u32[]{:S(2)}) async-start(bf16[16,2,12288]{2,1,0:T(2,128)(2,1)} %reshape.616), calls=%async_computation.20 | async-start | bytes 1572864 | tf_op jit(solution)/shard_map/all_to_all | solution.py:77
  94.6 28.3 %all-to-all-start.6 = ((bf16[16,32,1024]{2,1,0:T(8,128)(2,1)}), bf16[16,32,1024]{2,1,0:T(8,128)(2,1)S(1)}, u32[]{:S(2)}, u32[]{:S(2)}) async-start(bf16[16,32,1024]{2,1,0:T(8,128)(2,1)} %bitcast.13), calls=%async_computation.6 | async-start | bytes 2097152 | tf_op jit(solution)/shard_map/all_to_all | solution.py:160
  122.8 29.7 %all-to-all-start.10 = ((bf16[16,32,1024]{2,1,0:T(8,128)(2,1)}), bf16[16,32,1024]{2,1,0:T(8,128)(2,1)S(1)}, u32[]{:S(2)}, u32[]{:S(2)}) async-start(bf16[16,32,1024]{2,1,0:T(8,128)(2,1)} %bitcast.25), calls=%async_computation.10 | async-start | bytes 2097152 | tf_op jit(solution)/shard_map/all_to_all | solution.py:186
  152.5 29.8 %all-to-all-start = ((bf16[16,32,1024]{2,1,0:T(8,128)(2,1)}), bf16[16,32,1024]{2,1,0:T(8,128)(2,1)S(1)}, u32[]{:S(2)}, u32[]{:S(2)}) async-start(bf16[16,32,1024]{2,1,0:T(8,128)(2,1)} %bitcast.3), calls=%async_computation | async-start | bytes 2097152 | tf_op jit(solution)/shard_map/all_to_all | solution.py:160
  183.3 29.8 %all-to-all-start.8 = ((bf16[16,32,1024]{2,1,0:T(8,128)(2,1)}), bf16[16,32,1024]{2,1,0:T(8,128)(2,1)}, u32[]{:S(2)}, u32[]{:S(2)}) async-start(bf16[16,32,1024]{2,1,0:T(8,128)(2,1)} %bitcast.19), calls=%async_computation.8 | async-start | bytes 2097152 | tf_op jit(solution)/shard_map/all_to_all | solution.py:186
  213.1 38.6 %all-to-all-start.1 = ((bf16[16,2,24576]{2,1,0:T(2,128)(2,1)}), bf16[16,2,24576]{2,1,0:T(2,128)(2,1)S(1)}, u32[]{:S(2)}, u32[]{:S(2)}) async-start(bf16[16,2,24576]{2,1,0:T(2,128)(2,1)} %reshape.600), calls=%async_computation.1 | async-start | bytes 3145728 | tf_op jit(solution)/shard_map/all_to_all | solution.py:37
  251.8 31.3 %all-to-all-start.4 = ((bf16[16,2,12288]{2,1,0:T(2,128)(2,1)}), bf16[16,2,12288]{2,1,0:T(2,128)(2,1)}, u32[]{:S(2)}, u32[]{:S(2)}) async-start(bf16[16,2,12288]{2,1,0:T(2,128)(2,1)} %reshape.606), calls=%async_computation.4 | async-start | bytes 1572864 | tf_op jit(solution)/shard_map/all_to_all | solution.py:48
  283.1 46.9 %all-to-all-start.12 = ((bf16[16,2,24576]{2,1,0:T(2,128)(2,1)}), bf16[16,2,24576]{2,1,0:T(2,128)(2,1)}, u32[]{:S(2)}, u32[]{:S(2)}) async-start(bf16[16,2,24576]{2,1,0:T(2,128)(2,1)} %reshape.612), calls=%async_computation.12 | async-start | bytes 3145728 | tf_op jit(solution)/shard_map/all_to_all | solution.py:56
  330.0 38.1 %all-to-all-start.14 = ((bf16[16,2,24576]{2,1,0:T(2,128)(2,1)}), bf16[16,2,24576]{2,1,0:T(2,128)(2,1)S(1)}, u32[]{:S(2)}, u32[]{:S(2)}) async-start(bf16[16,2,24576]{2,1,0:T(2,128)(2,1)} %reshape.608), calls=%async_computation.15 | async-start | bytes 3145728 | tf_op jit(solution)/shard_map/all_to_all | solution.py:63
  368.1 41.0 %all-to-all-start.2 = ((bf16[16,2,24576]{2,1,0:T(2,128)(2,1)}), bf16[16,2,24576]{2,1,0:T(2,128)(2,1)S(1)}, u32[]{:S(2)}, u32[]{:S(2)}) async-start(bf16[16,2,24576]{2,1,0:T(2,128)(2,1)} %reshape.602), calls=%async_computation.2 | async-start | bytes 3145728 | tf_op jit(solution)/shard_map/all_to_all | solution.py:47
  409.0 65.5 %all-to-all-start.19 = ((bf16[16,2,12288]{2,1,0:T(2,128)(2,1)}), bf16[16,2,12288]{2,1,0:T(2,128)(2,1)}, u32[]{:S(2)}, u32[]{:S(2)}) async-start(bf16[16,2,12288]{2,1,0:T(2,128)(2,1)} %reshape.618), calls=%async_computation.21 | async-start | bytes 1572864 | tf_op jit(solution)/shard_map/all_to_all | solution.py:90
  418.2 129.4 %all-gather.3.cloned.1.call-start = ((), (), s32[]{:S(2)}) async-start(), calls=%async_computation.22 | async-start | bytes 4718592 | tf_op jit(solution)/shard_map/all_gather | solution.py:141
  474.5 25.1 %all-to-all-start.17 = ((bf16[16,2,12288]{2,1,0:T(2,128)(2,1)}), bf16[16,2,12288]{2,1,0:T(2,128)(2,1)}, u32[]{:S(2)}, u32[]{:S(2)}) async-start(bf16[16,2,12288]{2,1,0:T(2,128)(2,1)} %reshape.622), calls=%async_computation.18 | async-start | bytes 1572864 | tf_op jit(solution)/shard_map/all_to_all | solution.py:89
  499.6 37.2 %all-to-all-start.15 = ((bf16[16,2,24576]{2,1,0:T(2,128)(2,1)}), bf16[16,2,24576]{2,1,0:T(2,128)(2,1)S(1)}, u32[]{:S(2)}, u32[]{:S(2)}) async-start(bf16[16,2,24576]{2,1,0:T(2,128)(2,1)} %reshape.610), calls=%async_computation.16 | async-start | bytes 3145728 | tf_op jit(solution)/shard_map/all_to_all | solution.py:88
  505.0 48.3 %all-gather.5.cloned.1.call-start = ((), (), s32[]{:S(2)}) async-start(), calls=%async_computation.23 | async-start | bytes 2359296 | tf_op jit(solution)/shard_map/all_gather | solution.py:142
  538.0 41.0 %all-to-all-start.13 = ((bf16[16,2,24576]{2,1,0:T(2,128)(2,1)}), bf16[16,2,24576]{2,1,0:T(2,128)(2,1)S(1)}, u32[]{:S(2)}, u32[]{:S(2)}) async-start(bf16[16,2,24576]{2,1,0:T(2,128)(2,1)} %reshape.614), calls=%async_computation.13 | async-start | bytes 3145728 | tf_op jit(solution)/shard_map/all_to_all | solution.py:87
  547.1 224.7 %reduce-scatter.5.cloned.1.call-start = ((), (), s32[]{:S(2)}) async-start(), calls=%async_computation.25 | async-start | bytes 2359296 | tf_op jit(solution)/shard_map/reduce_scatter | solution.py:227
  580.1 32.0 %all-to-all-start.11 = ((bf16[16,32,1024]{2,1,0:T(8,128)(2,1)}), bf16[16,32,1024]{2,1,0:T(8,128)(2,1)S(1)}, u32[]{:S(2)}, u32[]{:S(2)}) async-start(bf16[16,32,1024]{2,1,0:T(8,128)(2,1)} %bitcast.126), calls=%async_computation.11 | async-start | bytes 2097152 | tf_op jit(solution)/shard_map/all_to_all | solution.py:212
  612.1 29.7 %all-to-all-start.7 = ((bf16[16,32,1024]{2,1,0:T(8,128)(2,1)}), bf16[16,32,1024]{2,1,0:T(8,128)(2,1)S(1)}, u32[]{:S(2)}, u32[]{:S(2)}) async-start(bf16[16,32,1024]{2,1,0:T(8,128)(2,1)} %bitcast.125), calls=%async_computation.7 | async-start | bytes 2097152 | tf_op jit(solution)/shard_map/all_to_all | solution.py:168
  618.9 158.3 %reduce-scatter.3.cloned.1.call-start = ((), (), s32[]{:S(2)}) async-start(), calls=%async_computation.24 | async-start | bytes 4718592 | tf_op jit(solution)/shard_map/reduce_scatter | solution.py:224
  641.8 31.1 %all-to-all-start.9 = ((bf16[16,32,1024]{2,1,0:T(8,128)(2,1)}), bf16[16,32,1024]{2,1,0:T(8,128)(2,1)S(1)}, u32[]{:S(2)}, u32[]{:S(2)}) async-start(bf16[16,32,1024]{2,1,0:T(8,128)(2,1)} %bitcast.124), calls=%async_computation.9 | async-start | bytes 2097152 | tf_op jit(solution)/shard_map/all_to_all | solution.py:212
  672.9 80.7 %all-to-all-start.5 = ((bf16[16,32,1024]{2,1,0:T(8,128)(2,1)}), bf16[16,32,1024]{2,1,0:T(8,128)(2,1)}, u32[]{:S(2)}, u32[]{:S(2)}) async-start(bf16[16,32,1024]{2,1,0:T(8,128)(2,1)} %bitcast.123), calls=%async_computation.5 | async-start | bytes 2097152 | tf_op jit(solution)/shard_map/all_to_all | solution.py:168
  (55 other events, 335.4 us)
Sparse Core Ops, SparseCore 0:
  474.6 46.1 all-gather.2
  522.4 27.1 all-gather.4
  569.3 27.4 reduce-scatter.4
  626.6 44.7 reduce-scatter.2
where the time goes:
time: 803 us; the launch traced here: 793 us
  waiting for transfers between devices  219 us (27%)
  local copies, waits for them, and re-layouts  202 us (25%)
  other arithmetic  170 us (21%)
  starting transfers between devices  142 us (18%)
  matrix products  45.1 us (6%)
  between operations  15.1 us (2%)
    unnamed x136, local copies, waits for them, and re-layouts  109 us
    all_to_all x2, waiting for transfers between devices, on_device(): lax.all_to_all(outgoing.reshape(count, capacity, width), 'expert', split_...  30.3 us
    all_to_all x1, waiting for transfers between devices, relocate_weights(): lax.all_to_all(pair[0].reshape(count, -1), 'expert', split_axis=0, concat...  29 us
    all_to_all x1, waiting for transfers between devices, relocate_moments(): lax.all_to_all(group[1].reshape(count, -1).astype(jnp.bfloat16), 'expert'...  25.1 us
    all_to_all x1, waiting for transfers between devices, relocate_weights(): lax.all_to_all(picked_first, 'expert', split_axis=0, concat_axis=0, tiled...  23.4 us
    convert_element_type x2, other arithmetic, adam_update(): second_new = beta_two * second + (1.0 - beta_two) * gradient * gradient  19.9 us
    convert_element_type x2, other arithmetic, adam_update(): first_new = beta_one * first + (1.0 - beta_one) * gradient  19.8 us
    all_to_all x2, waiting for transfers between devices, on_device(): lax.all_to_all(token_part.reshape(count, capacity, width), 'expert', spli...  19.3 us
  transfers between devices with their start and end apart: 24, of which 15 were waited for; matrix products, arithmetic and copies ran while one was open for 48% of the time, Pallas kernels for 0%

commit v1 on v0

v1 whole, which is shorter than its diff:
```python
import jax
import jax.numpy as jnp
from jax import lax
from jax.sharding import PartitionSpec as P

beta_one = 0.9
beta_two = 0.95
learn_rate = 0.00042
decay_rate = 0.1
epsilon = 1e-08
steps_done = 10


def adam_update(weight, gradient, first, second):
    first_new = beta_one * first + (1.0 - beta_one) * gradient
    second_new = beta_two * second + (1.0 - beta_two) * gradient * gradient
    ratio = (
        first_new
        / (1.0 - beta_one**steps_done)
        / (jnp.sqrt(second_new / (1.0 - beta_two**steps_done)) + epsilon)
    )
    master = weight.astype(jnp.float32)
    return (
        (master - learn_rate * (ratio + decay_rate * master)).astype(jnp.bfloat16),
        first_new,
        second_new,
    )


def spread_pieces(block, count):
    rows = block.shape[1] // count
    pieces = block.astype(jnp.bfloat16).reshape(count, rows, block.shape[2])
    return lax.all_to_all(pieces, "expert", split_axis=0, concat_axis=0, tiled=True)


def land_pieces(spread, expert_plan, shape):
    picked = jnp.take(spread, expert_plan, axis=0, mode="clip")
    return lax.all_to_all(picked, "expert", split_axis=0, concat_axis=0, tiled=True).reshape(shape)


def on_device(
    tokens,
    routes,
    gate_weights,
    cotangent,
    expert_plan,
    weight_in,
    weight_out,
    first_in,
    second_in,
    first_out,
    second_out,
):
    count = lax.axis_size("expert")
    micro_count, token_count, width = tokens.shape
    top_count = routes.shape[2]
    row_count = micro_count * token_count

    own_routes = routes.reshape(row_count, top_count)
    own_gates = gate_weights.reshape(row_count, top_count)
    hits = own_routes[None, :, :] == expert_plan[:, None, None]
    sent_gates = jnp.sum(jnp.where(hits, own_gates[None, :, :], 0.0), axis=2)
    gate_column = lax.all_to_all(
        sent_gates, "expert", split_axis=0, concat_axis=0, tiled=True
    ).reshape(count * row_count, 1)
    rows = lax.all_gather(tokens.reshape(row_count, width), "expert", axis=0, tiled=True)
    upstream = lax.all_gather(cotangent.reshape(row_count, width), "expert", axis=0, tiled=True)

    spread_in = spread_pieces(weight_in, count)
    spread_out = spread_pieces(weight_out, count)
    own_in = land_pieces(spread_in, expert_plan, weight_in.shape)
    own_out = land_pieces(spread_out, expert_plan, weight_out.shape)
    whole_in = lax.all_gather(own_in[0], "dp", axis=0, tiled=True)
    whole_out = lax.all_gather(own_out[0], "dp", axis=0, tiled=True)
    hidden_width = whole_out.shape[0]

    moments = (first_in, second_in, first_out, second_out)
    spread_moments = [spread_pieces(member, count) for member in moments]
    landed = [
        land_pieces(spread, expert_plan, member.shape)
        for spread, member in zip(spread_moments, moments)
    ]

    pre = jnp.dot(rows, whole_in, preferred_element_type=jnp.float32)
    gate_part = pre[:, :hidden_width]
    up_part = pre[:, hidden_width:]
    sigma = jax.nn.sigmoid(gate_part)
    hidden = (gate_part * sigma * up_part).astype(jnp.bfloat16)
    output = jnp.dot(hidden, whole_out, preferred_element_type=jnp.float32)
    weighted = (gate_column * output).astype(jnp.bfloat16)
    layer_rows = lax.psum_scatter(weighted, "expert", scatter_dimension=0, tiled=True)

    scaled = (gate_column * upstream.astype(jnp.float32)).astype(jnp.bfloat16)
    hidden_grad = lax.dot_general(
        scaled, whole_out, (((1,), (1,)), ((), ())), preferred_element_type=jnp.float32
    )
    pre_grad = jnp.concatenate(
        [
            hidden_grad * up_part * sigma * (1.0 + gate_part * (1.0 - sigma)),
            hidden_grad * gate_part * sigma,
        ],
        axis=1,
    ).astype(jnp.bfloat16)
    grad_in = lax.dot_general(
        rows, pre_grad, (((0,), (0,)), ((), ())), preferred_element_type=jnp.float32
    ).astype(jnp.bfloat16)
    grad_out = lax.dot_general(
        hidden, scaled, (((0,), (0,)), ((), ())), preferred_element_type=jnp.float32
    ).astype(jnp.bfloat16)
    token_part = lax.dot_general(
        pre_grad, whole_in, (((1,), (1,)), ((), ())), preferred_element_type=jnp.float32
    ).astype(jnp.bfloat16)
    token_rows = lax.psum_scatter(token_part, "expert", scatter_dimension=0, tiled=True)
    share_in = lax.psum_scatter(grad_in, "dp", scatter_dimension=0, tiled=True)
    share_out = lax.psum_scatter(grad_out, "dp", scatter_dimension=0, tiled=True)

    first_in, second_in, first_out, second_out = [m.astype(jnp.float32) for m in landed]
    new_in, first_in_new, second_in_new = adam_update(
        own_in, share_in.astype(jnp.float32)[None], first_in, second_in
    )
    new_out, first_out_new, second_out_new = adam_update(
        own_out, share_out.astype(jnp.float32)[None], first_out, second_out
    )
    return (
        layer_rows.reshape(tokens.shape),
        token_rows.reshape(tokens.shape),
        new_in,
        new_out,
        first_in_new,
        second_in_new,
        first_out_new,
        second_out_new,
    )


def solution(mesh):
    placed = (
        P(None, ("expert", "dp"), None),
        P(None, ("expert", "dp"), None),
        P(None, ("expert", "dp"), None),
        P(None, ("expert", "dp"), None),
        P(),
        P("expert", "dp", None),
        P("expert", "dp", None),
        P("expert", "dp", None),
        P("expert", "dp", None),
        P("expert", "dp", None),
        P("expert", "dp", None),
    )
    return jax.shard_map(
        on_device,
        mesh=mesh,
        in_specs=placed,
        out_specs=(
            P(None, ("expert", "dp"), None),
            P(None, ("expert", "dp"), None),
            P("expert", "dp", None),
            P("expert", "dp", None),
            P("expert", "dp", None),
            P("expert", "dp", None),
            P("expert", "dp", None),
            P("expert", "dp", None),
        ),
        check_vma=False,
    )
```

time: 803 us -> 575 us (0.72)
  local copies, waits for them, and re-layouts: 202 us -> 28.8 us
  other arithmetic: 170 us -> 29.9 us
  blocking collectives: 0 us -> 105 us
  starting transfers between devices: 142 us -> 70.2 us
  waiting for transfers between devices: 219 us -> 259 us
  matrix products: 45.1 us -> 61.1 us
    all_to_all x0 -> x3, blocking collectives: none -> 105 us  [the longest x2 79.8 us: land_pieces(): lax.all_to_all(picked, 'expert', split_axis=0, concat_axis=0, tiled=True)]
    unnamed x136 -> x31, local copies, waits for them, and re-layouts: 109 us -> 12.3 us
    all_to_all x20 -> x10, starting transfers between devices: 141 us -> 69.7 us  [the longest x4 33.6 us: land_pieces(): lax.all_to_all(picked, 'expert', split_axis=0, concat_axis=0, tiled=True)]
    convert_element_type x15 -> x5, other arithmetic: 81 us -> 11.9 us  [the longest x4 6.52 us: spread_pieces(): pieces = block.astype(jnp.bfloat16).reshape(count, rows, block.shape[2])]
    all_gather x2 -> x4, waiting for transfers between devices: 0.02 us -> 57.2 us  [the longest x1 55.6 us: on_device(): lax.all_gather(cotangent.reshape(row_count, width), 'expert', axis=0, til...]
    all_to_all x10 -> x0, other arithmetic: 50.2 us -> none  [the longest x1 11.3 us: relocate_weights(): lax.all_to_all(pair[0].reshape(count, -1), 'expert', split_axis=0, concat...]
    convert_element_type x10 -> x0, local copies, waits for them, and re-layouts: 26.4 us -> none  [the longest x2 6.26 us: adam_update(): second_new = beta_two * second + (1.0 - beta_two) * gradient * gradient]
    gather x14 -> x6, local copies, waits for them, and re-layouts: 34.6 us -> 10 us  [land_pieces(): picked = jnp.take(spread, expert_plan, axis=0, mode='clip')]
  transfers between devices with their start and end apart: 24 -> 18, of which waited for: 15 -> 10; matrix products, arithmetic and copies ran while one was open for 48% -> 20% of each run, Pallas kernels for 0% -> 0%
where the time goes in v1:
time: 575 us; the launch traced here: 569 us
  waiting for transfers between devices  259 us (45%)
  blocking collectives  105 us (18%)
  starting transfers between devices  70.2 us (12%)
  matrix products  61.1 us (11%)
  other arithmetic  29.9 us (5%)
  local copies, waits for them, and re-layouts  28.8 us (5%)
  between operations  14.4 us (3%)
    all_to_all x4, waiting for transfers between devices, land_pieces(): lax.all_to_all(picked, 'expert', split_axis=0, concat_axis=0, tiled=True)  111 us
    all_to_all x5, waiting for transfers between devices, spread_pieces(): lax.all_to_all(pieces, 'expert', split_axis=0, concat_axis=0, tiled=True)  89.8 us
    all_to_all x2, blocking collectives, land_pieces(): lax.all_to_all(picked, 'expert', split_axis=0, concat_axis=0, tiled=True)  79.8 us
    all_gather x1, waiting for transfers between devices, on_device(): lax.all_gather(cotangent.reshape(row_count, width), 'expert', axis=0, til...  55.6 us
    all_to_all x4, starting transfers between devices, land_pieces(): lax.all_to_all(picked, 'expert', split_axis=0, concat_axis=0, tiled=True)  33.6 us
    all_to_all x5, starting transfers between devices, spread_pieces(): lax.all_to_all(pieces, 'expert', split_axis=0, concat_axis=0, tiled=True)  32.2 us
    all_to_all x1, blocking collectives, spread_pieces(): lax.all_to_all(pieces, 'expert', split_axis=0, concat_axis=0, tiled=True)  25 us
    dot_general x1, matrix products, on_device(): pre = jnp.dot(rows, whole_in, preferred_element_type=jnp.float32)  12.6 us
  transfers between devices with their start and end apart: 18, of which 10 were waited for; matrix products, arithmetic and copies ran while one was open for 20% of the time, Pallas kernels for 0%

profile of v1, /device:TPU:0, one launch (start us, length us, event | category | flops | bytes accessed | tf_op | source)
XLA Modules:
  0.0 568.6 jit_solution(558237692314014566)
XLA Ops:
  7.9 7.4 %all-to-all-start.1 = ((bf16[16,32,1536]{2,1,0:T(8,128)(2,1)}), bf16[16,32,1536]{2,1,0:T(8,128)(2,1)S(1)}, u32[]{:S(2)}, u32[]{:S(2)}) async-start(bf16[16,32,1536]{2,1,0:T(8,128)(2,1)} %bitcast.57), calls=%async_computation.1 | async-start | bytes 3145728 | tf_op jit(solution)/shard_map/all_to_all | solution.py:33
  15.4 40.2 %all-to-all-done.1 = bf16[16,32,1536]{2,1,0:T(8,128)(2,1)S(1)} async-done(((bf16[16,32,1536]{2,1,0:T(8,128)(2,1)}), bf16[16,32,1536]{2,1,0:T(8,128)(2,1)S(1)}, u32[]{:S(2)}, u32[]{:S(2)}) %all-to-all-start.1) | async-done | bytes 1572896 | tf_op jit(solution)/shard_map/all_to_all | solution.py:33
  56.2 55.8 %all_to_all.69 = bf16[16,32,1536]{2,1,0:T(8,128)(2,1)} all-to-all(bf16[16,32,1536]{2,1,0:T(8,128)(2,1)S(1)} %gather_fusion), channel_id=1, replica_groups=mesh['expert'=16,'dp'=2] {'expert'}, dimensions={0} | all-to-all | bytes 3145728 | tf_op jit(solution)/shard_map/all_to_all | solution.py:38
  112.2 25.0 %all_to_all.70 = bf16[16,24,1024]{2,1,0:T(8,128)(2,1)S(1)} all-to-all(bf16[16,24,1024]{2,1,0:T(8,128)(2,1)S(1)} %bitcast.60), channel_id=1, replica_groups=mesh['expert'=16,'dp'=2] {'expert'}, dimensions={0} | all-to-all | bytes 1572864 | tf_op jit(solution)/shard_map/all_to_all | solution.py:33
  137.8 24.0 %all_to_all.71 = bf16[16,24,1024]{2,1,0:T(8,128)(2,1)} all-to-all(bf16[16,24,1024]{2,1,0:T(8,128)(2,1)S(1)} %gather_fusion.1), channel_id=1, replica_groups=mesh['expert'=16,'dp'=2] {'expert'}, dimensions={0} | all-to-all | bytes 1572864 | tf_op jit(solution)/shard_map/all_to_all | solution.py:38
  168.2 12.6 %convolution_bitcast_fusion = f32[2048,1536]{0,1:T(8,128)} fusion(bf16[1024,1536]{1,0:T(8,128)(2,1)} %all-gather.5.cloned.1.call-done, bf16[2048,1024]{1,0:T(8,128)(2,1)} %all-gather.7.cloned.1.call-done), kind=kOutput, calls=%fused_computation.6 | convolution fusion | flops 6442450944 | bytes 19922944 | tf_op jit(solution)/shard_map/dot_general | solution.py:84
  180.8 6.0 %all-to-all-start.11 = ((bf16[16,24,1024]{2,1,0:T(8,128)(2,1)}), bf16[16,24,1024]{2,1,0:T(8,128)(2,1)S(1)}, u32[]{:S(2)}, u32[]{:S(2)}) async-start(bf16[16,24,1024]{2,1,0:T(8,128)(2,1)} %bitcast.20), calls=%async_computation.15 | async-start | bytes 1572864 | tf_op jit(solution)/shard_map/all_to_all | solution.py:33
  188.4 55.6 %all-gather.11.cloned.1.call-done = bf16[2048,1024]{1,0:T(8,128)(2,1)} async-done(((bf16[128,1024]{1,0:T(8,128)(2,1)}), bf16[2048,1024]{1,0:T(8,128)(2,1)}) %all-gather.11.cloned.1.call-update) | async-done | bytes 4194320 | tf_op jit(solution)/shard_map/all_gather | solution.py:67
  244.1 12.6 %multiply_convert_fusion.3 = (bf16[2048,768]{0,1:T(8,128)(2,1)}, bf16[2048,768]{0,1:T(8,128)(2,1)}, bf16[2048,768]{0,1:T(8,128)(2,1)S(1)}) fusion(f32[2048,1536]{0,1:T(8,128)} %convolution_bitcast_fusion, bf16[768,1024]{1,0:T(8,128)(2,1)} %all-gather.9.cloned.1.call-done, bf16[2048,1024]{1,0:T(8,128)(2,1)} %all-gather.11.cloned.1.call-done, ...), kind=kOutput, calls=%fused_computation.11 | convolution fusion | flops 3252682752 | bytes 27795456 | tf_op jit(solution)/shard_map/dot_general | solution.py:94
  268.7 11.6 %fusion.4 = bf16[1024,1536]{0,1:T(8,128)(2,1)} fusion(bf16[2048,1024]{1,0:T(8,128)(2,1)} %all-gather.7.cloned.1.call-done, bf16[2048,768]{0,1:T(8,128)(2,1)} %get-tuple-element.44, bf16[2048,768]{0,1:T(8,128)(2,1)} %get-tuple-element.43), kind=kOutput, calls=%fused_computation.22 | convolution fusion | flops 6456606720 | bytes 13631488 | tf_op jit(solution)/shard_map/dot_general | solution.py:104
  295.7 28.6 %all-to-all-done.5 = bf16[16,32,1536]{2,1,0:T(8,128)(2,1)S(1)} async-done(((bf16[16,32,1536]{2,1,0:T(8,128)(2,1)}), bf16[16,32,1536]{2,1,0:T(8,128)(2,1)S(1)}, u32[]{:S(2)}, u32[]{:S(2)}) %all-to-all-start.5) | async-done | bytes 1572896 | tf_op jit(solution)/shard_map/all_to_all | solution.py:33
  324.3 9.1 %all-to-all-start.7 = ((bf16[16,32,1536]{2,1,0:T(8,128)(2,1)}), bf16[16,32,1536]{2,1,0:T(8,128)(2,1)S(1)}, u32[]{:S(2)}, u32[]{:S(2)}) async-start(bf16[16,32,1536]{2,1,0:T(8,128)(2,1)} %bitcast.56), calls=%async_computation.10 | async-start | bytes 3145728 | tf_op jit(solution)/shard_map/all_to_all | solution.py:33
  333.5 11.8 %fusion.2 = bf16[2048,1024]{1,0:T(8,128)(2,1)} fusion(bf16[1024,1536]{1,0:T(8,128)(2,1)} %all-gather.5.cloned.1.call-done, bf16[2048,768]{0,1:T(8,128)(2,1)} %get-tuple-element.44, bf16[2048,768]{0,1:T(8,128)(2,1)} %get-tuple-element.43), kind=kOutput, calls=%fused_computation.20 | convolution fusion | flops 6457131008 | bytes 13631488 | tf_op jit(solution)/shard_map/dot_general | solution.py:110
  347.9 17.4 %all-to-all-done.7 = bf16[16,32,1536]{2,1,0:T(8,128)(2,1)S(1)} async-done(((bf16[16,32,1536]{2,1,0:T(8,128)(2,1)}), bf16[16,32,1536]{2,1,0:T(8,128)(2,1)S(1)}, u32[]{:S(2)}, u32[]{:S(2)}) %all-to-all-start.7) | async-done | bytes 1572896 | tf_op jit(solution)/shard_map/all_to_all | solution.py:33
  365.3 9.2 %all-to-all-start.12 = ((bf16[16,24,1024]{2,1,0:T(8,128)(2,1)}), bf16[16,24,1024]{2,1,0:T(8,128)(2,1)}, u32[]{:S(2)}, u32[]{:S(2)}) async-start(bf16[16,24,1024]{2,1,0:T(8,128)(2,1)} %gather_fusion.5), calls=%async_computation.16 | async-start | bytes 1572864 | tf_op jit(solution)/shard_map/all_to_all | solution.py:38
  377.1 28.5 %all-to-all-done.12 = bf16[16,24,1024]{2,1,0:T(8,128)(2,1)} async-done(((bf16[16,24,1024]{2,1,0:T(8,128)(2,1)}), bf16[16,24,1024]{2,1,0:T(8,128)(2,1)}, u32[]{:S(2)}, u32[]{:S(2)}) %all-to-all-start.12) | async-done | bytes 786464 | tf_op jit(solution)/shard_map/all_to_all | solution.py:38
  405.6 9.8 %all-to-all-start.10 = ((bf16[16,24,1024]{2,1,0:T(8,128)(2,1)}), bf16[16,24,1024]{2,1,0:T(8,128)(2,1)}, u32[]{:S(2)}, u32[]{:S(2)}) async-start(bf16[16,24,1024]{2,1,0:T(8,128)(2,1)} %gather_fusion.4), calls=%async_computation.13 | async-start | bytes 1572864 | tf_op jit(solution)/shard_map/all_to_all | solution.py:38
  417.2 25.2 %all-to-all-done.10 = bf16[16,24,1024]{2,1,0:T(8,128)(2,1)} async-done(((bf16[16,24,1024]{2,1,0:T(8,128)(2,1)}), bf16[16,24,1024]{2,1,0:T(8,128)(2,1)}, u32[]{:S(2)}, u32[]{:S(2)}) %all-to-all-start.10) | async-done | bytes 786464 | tf_op jit(solution)/shard_map/all_to_all | solution.py:38
  442.4 5.5 all-to-all-start.6
  448.0 7.9 %multiply_convert_fusion.1 = bf16[2048,1024]{1,0:T(8,128)(2,1)} fusion(bf16[2048,768]{0,1:T(8,128)(2,1)} %copy-done.13, bf16[768,1024]{1,0:T(8,128)(2,1)} %all-gather.9.cloned.1.call-done, f32[2048]{0:T(1024)S(1)} %bitcast.65), kind=kOutput, calls=%fused_computation.8 | convolution fusion | flops 3225419776 | bytes 8921088 | tf_op jit(solution)/shard_map/dot_general | solution.py:89
  457.7 22.1 %all-to-all-done.6 = bf16[16,32,1536]{2,1,0:T(8,128)(2,1)S(1)} async-done(((bf16[16,32,1536]{2,1,0:T(8,128)(2,1)}), bf16[16,32,1536]{2,1,0:T(8,128)(2,1)S(1)}, u32[]{:S(2)}, u32[]{:S(2)}) %all-to-all-start.6) | async-done | bytes 1572896 | tf_op jit(solution)/shard_map/all_to_all | solution.py:38
  479.8 9.2 %all-to-all-start.8 = ((bf16[16,32,1536]{2,1,0:T(8,128)(2,1)}), bf16[16,32,1536]{2,1,0:T(8,128)(2,1)}, u32[]{:S(2)}, u32[]{:S(2)}) async-start(bf16[16,32,1536]{2,1,0:T(8,128)(2,1)} %gather_fusion.3), calls=%async_computation.11 | async-start | bytes 3145728 | tf_op jit(solution)/shard_map/all_to_all | solution.py:38
  499.7 35.2 %all-to-all-done.8 = bf16[16,32,1536]{2,1,0:T(8,128)(2,1)} async-done(((bf16[16,32,1536]{2,1,0:T(8,128)(2,1)}), bf16[16,32,1536]{2,1,0:T(8,128)(2,1)}, u32[]{:S(2)}, u32[]{:S(2)}) %all-to-all-start.8) | async-done | bytes 1572896 | tf_op jit(solution)/shard_map/all_to_all | solution.py:38
  544.5 8.7 %fusion.11 = (f32[1,512,1536]{1,2,0:T(8,128)}, bf16[1,512,1536]{1,2,0:T(8,128)(2,1)}, f32[1,512,1536]{1,2,0:T(8,128)}) fusion(f32[512,1536]{0,1:T(8,128)} %copy.43, bf16[512,1536]{0,1:T(8,128)(2,1)} %reduce-scatter.9.cloned.1.call-done, f32[512,1536]{0,1:T(8,128)S(1)} %copy-done.1, bf16[512,1536]{0,1:T(8,128)(2,1)} %copy.41), kind=kLoop, calls=%fused_computation.35 | loop fusion | flops 12582912 | bytes 17301504 | tf_op jit(solution)/shard_map/add | solution.py:16
  (83 shorter events, 75.4 us)
Async XLA Ops:
  7.2 161.0 %all-gather.7.cloned.1.call-start = ((), (), s32[]{:S(2)}) async-start(), calls=%async_computation.18 | async-start | bytes 4456448 | tf_op jit(solution)/shard_map/all_gather | solution.py:66
  7.9 47.7 %all-to-all-start.1 = ((bf16[16,32,1536]{2,1,0:T(8,128)(2,1)}), bf16[16,32,1536]{2,1,0:T(8,128)(2,1)S(1)}, u32[]{:S(2)}, u32[]{:S(2)}) async-start(bf16[16,32,1536]{2,1,0:T(8,128)(2,1)} %bitcast.57), calls=%async_computation.1 | async-start | bytes 3145728 | tf_op jit(solution)/shard_map/all_to_all | solution.py:33
  15.3 152.9 %all-gather.5.cloned.1.call-start = ((), (), s32[]{:S(2)}) async-start(), calls=%async_computation.17 | async-start | bytes 4718592 | tf_op jit(solution)/shard_map/all_gather | solution.py:73
  56.2 56.0 %copy-start.8 = (bf16[1,384,1024]{2,1,0:T(8,128)(2,1)S(1)}, bf16[1,384,1024]{2,1,0:T(8,128)(2,1)}, u32[]{:S(2)}) copy-start(bf16[1,384,1024]{2,1,0:T(8,128)(2,1)} %param.17) | copy-start | bytes 2359300
  112.1 50.3 %copy-start.9 = (f32[2,64,6]{1,0,2:T(2,128)S(1)}, f32[2,64,6]{1,0,2:T(2,128)}, u32[]{:S(2)}) copy-start(f32[2,64,6]{1,0,2:T(2,128)} %param.13) | copy-start | bytes 9220
  112.1 50.4 %copy-start.10 = (s32[2,64,6]{1,0,2:T(2,128)S(1)}, s32[2,64,6]{1,0,2:T(2,128)}, u32[]{:S(2)}) copy-start(s32[2,64,6]{1,0,2:T(2,128)} %param.12) | copy-start | bytes 9220
  112.1 55.1 %copy-start.6 = (f32[1,384,1024]{2,1,0:T(8,128)S(1)}, f32[1,384,1024]{2,1,0:T(8,128)}, u32[]{:S(2)}) copy-start(f32[1,384,1024]{2,1,0:T(8,128)} %param.21) | copy-start | bytes 4718596
  112.1 76.3 %all-gather.9.cloned.1.call-start = ((), (), s32[]{:S(2)}) async-start(), calls=%async_computation.19 | async-start | bytes 2359296 | tf_op jit(solution)/shard_map/all_gather | solution.py:74
  161.8 82.2 %all-gather.11.cloned.1.call-start = ((), (), s32[]{:S(2)}) async-start(), calls=%async_computation.21 | async-start | bytes 4456448 | tf_op jit(solution)/shard_map/all_gather | solution.py:67
  163.2 17.6 %all-to-all-start = ((f32[16,1,128]{2,1,0:T(1,128)}), f32[16,1,128]{2,1,0:T(1,128)S(1)}, u32[]{:S(2)}, u32[]{:S(2)}) async-start(f32[16,1,128]{2,1,0:T(1,128)} %bitcast.1), calls=%async_computation | async-start | bytes 16384 | tf_op jit(solution)/shard_map/all_to_all | solution.py:63
  180.8 83.4 %all-to-all-start.11 = ((bf16[16,24,1024]{2,1,0:T(8,128)(2,1)}), bf16[16,24,1024]{2,1,0:T(8,128)(2,1)S(1)}, u32[]{:S(2)}, u32[]{:S(2)}) async-start(bf16[16,24,1024]{2,1,0:T(8,128)(2,1)} %bitcast.20), calls=%async_computation.15 | async-start | bytes 1572864 | tf_op jit(solution)/shard_map/all_to_all | solution.py:33
  186.8 352.2 %reduce-scatter.11.cloned.1.call-start = ((), (), s32[]{:S(2)}) async-start(), calls=%async_computation.24 | async-start | bytes 2359296 | tf_op jit(solution)/shard_map/reduce_scatter | solution.py:115
  244.1 14.3 %copy-start.12 = (bf16[2048,1024]{1,0:T(8,128)(2,1)S(1)}, bf16[2048,1024]{1,0:T(8,128)(2,1)}, u32[]{:S(2)}) copy-start(bf16[2048,1024]{1,0:T(8,128)(2,1)} %all-gather.11.cloned.1.call-done) | copy-start | bytes 12582916
  264.2 23.0 %all-to-all-start.9 = ((bf16[16,24,1024]{2,1,0:T(8,128)(2,1)}), bf16[16,24,1024]{2,1,0:T(8,128)(2,1)}, u32[]{:S(2)}, u32[]{:S(2)}) async-start(bf16[16,24,1024]{2,1,0:T(8,128)(2,1)} %bitcast.18), calls=%async_computation.12 | async-start | bytes 1572864 | tf_op jit(solution)/shard_map/all_to_all | solution.py:33
  268.5 276.0 %reduce-scatter.9.cloned.1.call-start = ((), (), s32[]{:S(2)}) async-start(), calls=%async_computation.23 | async-start | bytes 4718592 | tf_op jit(solution)/shard_map/reduce_scatter | solution.py:114
  287.2 37.2 %all-to-all-start.5 = ((bf16[16,32,1536]{2,1,0:T(8,128)(2,1)}), bf16[16,32,1536]{2,1,0:T(8,128)(2,1)S(1)}, u32[]{:S(2)}, u32[]{:S(2)}) async-start(bf16[16,32,1536]{2,1,0:T(8,128)(2,1)} %bitcast.12), calls=%async_computation.7 | async-start | bytes 3145728 | tf_op jit(solution)/shard_map/all_to_all | solution.py:33
  324.3 41.0 %all-to-all-start.7 = ((bf16[16,32,1536]{2,1,0:T(8,128)(2,1)}), bf16[16,32,1536]{2,1,0:T(8,128)(2,1)S(1)}, u32[]{:S(2)}, u32[]{:S(2)}) async-start(bf16[16,32,1536]{2,1,0:T(8,128)(2,1)} %bitcast.56), calls=%async_computation.10 | async-start | bytes 3145728 | tf_op jit(solution)/shard_map/all_to_all | solution.py:33
  333.5 228.3 %reduce-scatter.7.cloned.1.call-start = ((), (), s32[]{:S(2)}) async-start(), calls=%async_computation.22 | async-start | bytes 4456448 | tf_op jit(solution)/shard_map/reduce_scatter | solution.py:113
  365.3 40.3 %all-to-all-start.12 = ((bf16[16,24,1024]{2,1,0:T(8,128)(2,1)}), bf16[16,24,1024]{2,1,0:T(8,128)(2,1)}, u32[]{:S(2)}, u32[]{:S(2)}) async-start(bf16[16,24,1024]{2,1,0:T(8,128)(2,1)} %gather_fusion.5), calls=%async_computation.16 | async-start | bytes 1572864 | tf_op jit(solution)/shard_map/all_to_all | solution.py:38
  405.6 36.8 %all-to-all-start.10 = ((bf16[16,24,1024]{2,1,0:T(8,128)(2,1)}), bf16[16,24,1024]{2,1,0:T(8,128)(2,1)}, u32[]{:S(2)}, u32[]{:S(2)}) async-start(bf16[16,24,1024]{2,1,0:T(8,128)(2,1)} %gather_fusion.4), calls=%async_computation.13 | async-start | bytes 1572864 | tf_op jit(solution)/shard_map/all_to_all | solution.py:38
  442.4 37.3 %all-to-all-start.6 = ((bf16[16,32,1536]{2,1,0:T(8,128)(2,1)}), bf16[16,32,1536]{2,1,0:T(8,128)(2,1)S(1)}, u32[]{:S(2)}, u32[]{:S(2)}) async-start(bf16[16,32,1536]{2,1,0:T(8,128)(2,1)} %gather_fusion.2), calls=%async_computation.8 | async-start | bytes 3145728 | tf_op jit(solution)/shard_map/all_to_all | solution.py:38
  447.9 113.8 %reduce-scatter.5.cloned.1.call-start = ((), (), s32[]{:S(2)}) async-start(), calls=%async_computation.20 | async-start | bytes 4456448 | tf_op jit(solution)/shard_map/reduce_scatter | solution.py:91
  457.7 36.2 %copy-start = (bf16[16,32,1536]{2,1,0:T(8,128)(2,1)S(1)}, bf16[16,32,1536]{2,1,0:T(8,128)(2,1)}, u32[]{:S(2)}) copy-start(bf16[16,32,1536]{2,1,0:T(8,128)(2,1)} %all_to_all.69) | copy-start | bytes 4718596
  479.8 55.1 %all-to-all-start.8 = ((bf16[16,32,1536]{2,1,0:T(8,128)(2,1)}), bf16[16,32,1536]{2,1,0:T(8,128)(2,1)}, u32[]{:S(2)}, u32[]{:S(2)}) async-start(bf16[16,32,1536]{2,1,0:T(8,128)(2,1)} %gather_fusion.3), calls=%async_computation.11 | async-start | bytes 3145728 | tf_op jit(solution)/shard_map/all_to_all | solution.py:38
  (8 other events, 44.4 us)
Sparse Core Ops, SparseCore 0:
  10.1 83.2 all-gather.6
  112.2 45.1 all-gather.4
  161.9 26.4 all-gather.8
  190.5 53.5 all-gather.10
  263.3 24.6 reduce-scatter.10
  290.1 43.4 reduce-scatter.8
  345.4 97.0 reduce-scatter.6
  456.0 95.6 reduce-scatter.4

commit v2 on v1

--- a/solution.py
+++ b/solution.py
@@ -1,6 +1,7 @@
 import jax
 import jax.numpy as jnp
 from jax import lax
+from jax.experimental.layout import Layout, with_layout_constraint
 from jax.sharding import PartitionSpec as P
 
 beta_one = 0.9
@@ -27,15 +28,24 @@
     )
 
 
-def spread_pieces(block, count):
-    rows = block.shape[1] // count
-    pieces = block.astype(jnp.bfloat16).reshape(count, rows, block.shape[2])
+def exchange(pieces):
     return lax.all_to_all(pieces, "expert", split_axis=0, concat_axis=0, tiled=True)
 
 
-def land_pieces(spread, expert_plan, shape):
-    picked = jnp.take(spread, expert_plan, axis=0, mode="clip")
-    return lax.all_to_all(picked, "expert", split_axis=0, concat_axis=0, tiled=True).reshape(shape)
+def cut(block, count):
+    return block.astype(jnp.bfloat16).reshape(count, block.shape[1] // count, block.shape[2])
+
+
+def pick(spread, expert_plan):
+    return jnp.take(spread, expert_plan, axis=0, mode="clip")
+
+
+def tie(*values):
+    return lax.optimization_barrier(values)
+
+
+def row_major(value):
+    return with_layout_constraint(value, Layout(major_to_minor=tuple(range(value.ndim))))
 
 
 def on_device(
@@ -66,30 +76,29 @@
     rows = lax.all_gather(tokens.reshape(row_count, width), "expert", axis=0, tiled=True)
     upstream = lax.all_gather(cotangent.reshape(row_count, width), "expert", axis=0, tiled=True)
 
-    spread_in = spread_pieces(weight_in, count)
-    spread_out = spread_pieces(weight_out, count)
-    own_in = land_pieces(spread_in, expert_plan, weight_in.shape)
-    own_out = land_pieces(spread_out, expert_plan, weight_out.shape)
+    pieces, gate_column = tie(cut(weight_in, count), gate_column)
+    spread_in = exchange(pieces)
+    pieces, spread_in = tie(cut(weight_out, count), spread_in)
+    spread_out = exchange(pieces)
+    pieces, spread_out = tie(pick(spread_in, expert_plan), spread_out)
+    own_in = exchange(pieces).reshape(weight_in.shape)
+    pieces, own_in = tie(pick(spread_out, expert_plan), own_in)
+    own_out = exchange(pieces).reshape(weight_out.shape)
+    own_in, rows, upstream = tie(own_in, rows, upstream)
     whole_in = lax.all_gather(own_in[0], "dp", axis=0, tiled=True)
+    pieces, own_out = tie(cut(first_in, count), own_out)
     whole_out = lax.all_gather(own_out[0], "dp", axis=0, tiled=True)
     hidden_width = whole_out.shape[0]
 
-    moments = (first_in, second_in, first_out, second_out)
-    spread_moments = [spread_pieces(member, count) for member in moments]
-    landed = [
-        land_pieces(spread, expert_plan, member.shape)
-        for spread, member in zip(spread_moments, moments)
-    ]
-
+    spread_one = exchange(pieces)
     pre = jnp.dot(rows, whole_in, preferred_element_type=jnp.float32)
+    pieces, spread_one, pre = tie(cut(second_in, count), spread_one, pre)
+    spread_two = exchange(pieces)
+
     gate_part = pre[:, :hidden_width]
     up_part = pre[:, hidden_width:]
     sigma = jax.nn.sigmoid(gate_part)
     hidden = (gate_part * sigma * up_part).astype(jnp.bfloat16)
-    output = jnp.dot(hidden, whole_out, preferred_element_type=jnp.float32)
-    weighted = (gate_column * output).astype(jnp.bfloat16)
-    layer_rows = lax.psum_scatter(weighted, "expert", scatter_dimension=0, tiled=True)
-
     scaled = (gate_column * upstream.astype(jnp.float32)).astype(jnp.bfloat16)
     hidden_grad = lax.dot_general(
         scaled, whole_out, (((1,), (1,)), ((), ())), preferred_element_type=jnp.float32
@@ -101,25 +110,57 @@
         ],
         axis=1,
     ).astype(jnp.bfloat16)
-    grad_in = lax.dot_general(
-        rows, pre_grad, (((0,), (0,)), ((), ())), preferred_element_type=jnp.float32
+    output = jnp.dot(hidden, whole_out, preferred_element_type=jnp.float32)
+    weighted = (gate_column * output).astype(jnp.bfloat16)
+    pieces, spread_two, weighted, late_in = tie(
+        cut(first_out, count), spread_two, weighted, whole_in
+    )
+    spread_three = exchange(pieces)
+    layer_rows = lax.psum_scatter(weighted, "expert", scatter_dimension=0, tiled=True)
+
+    token_part = lax.dot_general(
+        pre_grad, late_in, (((1,), (1,)), ((), ())), preferred_element_type=jnp.float32
     ).astype(jnp.bfloat16)
-    grad_out = lax.dot_general(
-        hidden, scaled, (((0,), (0,)), ((), ())), preferred_element_type=jnp.float32
-    ).astype(jnp.bfloat16)
-    token_part = lax.dot_general(
-        pre_grad, whole_in, (((1,), (1,)), ((), ())), preferred_element_type=jnp.float32
-    ).astype(jnp.bfloat16)
+    pieces, spread_three, token_part, late_rows = tie(
+        cut(second_out, count), spread_three, token_part, rows
+    )
+    spread_four = exchange(pieces)
     token_rows = lax.psum_scatter(token_part, "expert", scatter_dimension=0, tiled=True)
+    grad_in = row_major(
+        lax.dot_general(
+            late_rows, pre_grad, (((0,), (0,)), ((), ())), preferred_element_type=jnp.float32
+        ).astype(jnp.bfloat16)
+    )
+    pieces, spread_four, grad_in, late_upstream = tie(
+        pick(spread_one, expert_plan), spread_four, grad_in, upstream
+    )
+    landed_one = exchange(pieces)
     share_in = lax.psum_scatter(grad_in, "dp", scatter_dimension=0, tiled=True)
+    scaled = (gate_column * late_upstream.astype(jnp.float32)).astype(jnp.bfloat16)
+    grad_out = row_major(
+        lax.dot_general(
+            hidden, scaled, (((0,), (0,)), ((), ())), preferred_element_type=jnp.float32
+        ).astype(jnp.bfloat16)
+    )
+    pieces, landed_one, grad_out = tie(pick(spread_two, expert_plan), landed_one, grad_out)
+    landed_two = exchange(pieces)
     share_out = lax.psum_scatter(grad_out, "dp", scatter_dimension=0, tiled=True)
-
-    first_in, second_in, first_out, second_out = [m.astype(jnp.float32) for m in landed]
+    pieces, landed_two = tie(pick(spread_three, expert_plan), landed_two)
+    landed_three = exchange(pieces)
+    pieces, landed_three = tie(pick(spread_four, expert_plan), landed_three)
+    landed_four = exchange(pieces)
+
     new_in, first_in_new, second_in_new = adam_update(
-        own_in, share_in.astype(jnp.float32)[None], first_in, second_in
+        own_in,
+        share_in.astype(jnp.float32)[None],
+        landed_one.reshape(first_in.shape).astype(jnp.float32),
+        landed_two.reshape(second_in.shape).astype(jnp.float32),
     )
     new_out, first_out_new, second_out_new = adam_update(
-        own_out, share_out.astype(jnp.float32)[None], first_out, second_out
+        own_out,
+        share_out.astype(jnp.float32)[None],
+        landed_three.reshape(first_out.shape).astype(jnp.float32),
+        landed_four.reshape(second_out.shape).astype(jnp.float32),
     )
     return (
         layer_rows.reshape(tokens.shape),

time: 575 us -> 574 us (level)
  waiting for transfers between devices: 259 us -> 297 us
  blocking collectives: 105 us -> 72.2 us
  local copies, waits for them, and re-layouts: 28.8 us -> 18.3 us
  starting transfers between devices: 70.2 us -> 77.7 us
    reduce_scatter x1, waiting for transfers between devices: 0.01 us -> 76.3 us  [on_device(): lax.psum_scatter(token_part, 'expert', scatter_dimension=0, tiled=True)]
    all_gather x1, waiting for transfers between devices: 55.6 us -> 0.01 us  [on_device(): lax.all_gather(cotangent.reshape(row_count, width), 'expert', axis=0, til...]
    all_to_all x3 -> x2, blocking collectives: 105 us -> 72.2 us  [the longest x1 58.6 us: exchange(): lax.all_to_all(pieces, 'expert', split_axis=0, concat_axis=0, tiled=True)]
    reduce_scatter x1, waiting for transfers between devices: 0.01 us -> 16.9 us  [on_device(): lax.psum_scatter(weighted, 'expert', scatter_dimension=0, tiled=True)]
    all_to_all x10 -> x11, waiting for transfers between devices: 201 us -> 187 us  [exchange(): lax.all_to_all(pieces, 'expert', split_axis=0, concat_axis=0, tiled=True)]
    all_gather x1, waiting for transfers between devices: 0.01 us -> 13.2 us  [on_device(): whole_in = lax.all_gather(own_in[0], 'dp', axis=0, tiled=True)]
    add x1 -> x0, other arithmetic: 8.66 us -> none  [adam_update(): second_new = beta_two * second + (1.0 - beta_two) * gradient * gradient]
    unnamed x31 -> x24, local copies, waits for them, and re-layouts: 12.3 us -> 4.62 us
  transfers between devices with their start and end apart: 18 -> 19, of which waited for: 10 -> 15; matrix products, arithmetic and copies ran while one was open for 20% -> 19% of each run, Pallas kernels for 0% -> 0%
where the time goes in v2:
time: 574 us; the launch traced here: 572 us
  waiting for transfers between devices  297 us (52%)
  starting transfers between devices  77.7 us (14%)
  blocking collectives  72.2 us (13%)
  matrix products  61.8 us (11%)
  other arithmetic  30.9 us (5%)
  local copies, waits for them, and re-layouts  18.3 us (3%)
  between operations  14.3 us (2%)
    all_to_all x11, waiting for transfers between devices, exchange(): lax.all_to_all(pieces, 'expert', split_axis=0, concat_axis=0, tiled=True)  187 us
    all_to_all x11, starting transfers between devices, exchange(): lax.all_to_all(pieces, 'expert', split_axis=0, concat_axis=0, tiled=True)  77.3 us
    reduce_scatter x1, waiting for transfers between devices, on_device(): lax.psum_scatter(token_part, 'expert', scatter_dimension=0, tiled=True)  76.3 us
    all_to_all x1, blocking collectives, exchange(): lax.all_to_all(pieces, 'expert', split_axis=0, concat_axis=0, tiled=True)  58.6 us
    reduce_scatter x1, waiting for transfers between devices, on_device(): lax.psum_scatter(weighted, 'expert', scatter_dimension=0, tiled=True)  16.9 us
    all_to_all x1, blocking collectives, on_device(): lax.all_to_all(sent_gates, 'expert', split_axis=0, concat_axis=0, tiled=T...  13.6 us
    all_gather x1, waiting for transfers between devices, on_device(): whole_in = lax.all_gather(own_in[0], 'dp', axis=0, tiled=True)  13.2 us
    convert_element_type x2, other arithmetic, adam_update(): (master - learn_rate * (ratio + decay_rate * master)).astype(jnp.bfloat16)  13.1 us
  transfers between devices with their start and end apart: 19, of which 15 were waited for; matrix products, arithmetic and copies ran while one was open for 19% of the time, Pallas kernels for 0%

profile of v2, /device:TPU:0, one launch (start us, length us, event | category | flops | bytes accessed | tf_op | source)
XLA Modules:
  0.0 572.1 jit_solution(7056833329719316699)
XLA Ops:
  10.9 13.6 %all_to_all.69 = f32[16,1,128]{2,1,0:T(1,128)S(1)} all-to-all(f32[16,1,128]{2,1,0:T(1,128)S(1)} %bitcast.69), channel_id=1, replica_groups=mesh['expert'=16,'dp'=2] {'expert'}, dimensions={0} | all-to-all | bytes 16384 | tf_op jit(solution)/shard_map/all_to_all | solution.py:73
  24.6 58.6 %all_to_all.70 = bf16[16,32,1536]{2,1,0:T(8,128)(2,1)S(1)} all-to-all(bf16[16,32,1536]{2,1,0:T(8,128)(2,1)} %bitcast.64), channel_id=1, replica_groups=mesh['expert'=16,'dp'=2] {'expert'}, dimensions={0} | all-to-all | bytes 3145728 | tf_op jit(solution)/shard_map/all_to_all | solution.py:32
  89.9 25.1 %all-to-all-done.2 = bf16[16,24,1024]{2,1,0:T(8,128)(2,1)S(1)} async-done(((bf16[16,24,1024]{2,1,0:T(8,128)(2,1)}), bf16[16,24,1024]{2,1,0:T(8,128)(2,1)S(1)}, u32[]{:S(2)}, u32[]{:S(2)}) %all-to-all-start.2) | async-done | bytes 786464 | tf_op jit(solution)/shard_map/all_to_all | solution.py:32
  122.0 45.1 %all-to-all-done.3 = bf16[16,32,1536]{2,1,0:T(8,128)(2,1)S(1)} async-done(((bf16[16,32,1536]{2,1,0:T(8,128)(2,1)}), bf16[16,32,1536]{2,1,0:T(8,128)(2,1)S(1)}, u32[]{:S(2)}, u32[]{:S(2)}) %all-to-all-start.3) | async-done | bytes 1572896 | tf_op jit(solution)/shard_map/all_to_all | solution.py:32
  168.3 8.9 %all-to-all-start.4 = ((bf16[16,24,1024]{2,1,0:T(8,128)(2,1)}), bf16[16,24,1024]{2,1,0:T(8,128)(2,1)S(1)}, u32[]{:S(2)}, u32[]{:S(2)}) async-start(bf16[16,24,1024]{2,1,0:T(8,128)(2,1)} %gather_fusion.1), calls=%async_computation.4 | async-start | bytes 1572864 | tf_op jit(solution)/shard_map/all_to_all | solution.py:32
  180.5 15.3 %all-to-all-done.4 = bf16[16,24,1024]{2,1,0:T(8,128)(2,1)S(1)} async-done(((bf16[16,24,1024]{2,1,0:T(8,128)(2,1)}), bf16[16,24,1024]{2,1,0:T(8,128)(2,1)S(1)}, u32[]{:S(2)}, u32[]{:S(2)}) %all-to-all-start.4) | async-done | bytes 786464 | tf_op jit(solution)/shard_map/all_to_all | solution.py:32
  204.5 13.2 %all-gather.11.cloned.1.call-done = bf16[1,1024,1536]{2,1,0:T(8,128)(2,1)} async-done(((bf16[1,512,1536]{2,1,0:T(8,128)(2,1)}), bf16[1,1024,1536]{2,1,0:T(8,128)(2,1)}) %all-gather.11.cloned.1.call-update) | async-done | bytes 3145744 | tf_op jit(solution)/shard_map/all_gather | solution.py:88
  217.7 12.3 %fusion.23 = f32[2048,1536]{1,0:T(8,128)} fusion(bf16[2048,1024]{1,0:T(8,128)(2,1)} %all-gather.7.cloned.1.call-done, bf16[1,1024,1536]{2,1,0:T(8,128)(2,1)} %all-gather.11.cloned.1.call-done), kind=kOutput, calls=%fused_computation.51 | convolution fusion | flops 6442450944 | bytes 19922944 | tf_op jit(solution)/shard_map/dot_general | solution.py:94
  234.2 9.1 %all-to-all-start.6 = ((bf16[16,32,1536]{2,1,0:T(8,128)(2,1)}), bf16[16,32,1536]{2,1,0:T(8,128)(2,1)S(1)}, u32[]{:S(2)}, u32[]{:S(2)}) async-start(bf16[16,32,1536]{2,1,0:T(8,128)(2,1)} %bitcast.1), calls=%async_computation.6 | async-start | bytes 3145728 | tf_op jit(solution)/shard_map/all_to_all | solution.py:32
  246.8 12.8 %multiply_convert_fusion.4 = (bf16[2048,768]{1,0:T(8,128)(2,1)}, bf16[2048,768]{1,0:T(8,128)(2,1)}, bf16[2048,768]{1,0:T(8,128)(2,1)S(1)}) fusion(f32[2048,1536]{1,0:T(8,128)} %fusion.23, bf16[1,768,1024]{2,1,0:T(8,128)(2,1)} %all-gather.13.cloned.1.call-done, bf16[2048,1024]{1,0:T(8,128)(2,1)} %all-gather.9.cloned.1.call-done, f32[2048]{0:T(1024)S(1)} %bitcast.70), kind=kOutput, calls=%fused_computation.11 | convolution fusion | flops 3252682752 | bytes 27795456 | tf_op jit(solution)/shard_map/dot_general | solution.py:103
  266.2 8.9 %all-to-all-done.6 = bf16[16,32,1536]{2,1,0:T(8,128)(2,1)S(1)} async-done(((bf16[16,32,1536]{2,1,0:T(8,128)(2,1)}), bf16[16,32,1536]{2,1,0:T(8,128)(2,1)S(1)}, u32[]{:S(2)}, u32[]{:S(2)}) %all-to-all-start.6) | async-done | bytes 1572896 | tf_op jit(solution)/shard_map/all_to_all | solution.py:32
  275.1 9.2 %all-to-all-start.7 = ((bf16[16,24,1024]{2,1,0:T(8,128)(2,1)}), bf16[16,24,1024]{2,1,0:T(8,128)(2,1)}, u32[]{:S(2)}, u32[]{:S(2)}) async-start(bf16[16,24,1024]{2,1,0:T(8,128)(2,1)} %bitcast), calls=%async_computation.8 | async-start | bytes 1572864 | tf_op jit(solution)/shard_map/all_to_all | solution.py:32
  284.3 11.9 %fusion.6 = bf16[2048,1024]{1,0:T(8,128)(2,1)} fusion(bf16[1024,1536]{1,0:T(8,128)(2,1)} %bitcast.73, bf16[2048,768]{1,0:T(8,128)(2,1)} %get-tuple-element.85, bf16[2048,768]{1,0:T(8,128)(2,1)} %get-tuple-element.84), kind=kOutput, calls=%fused_computation.24 | convolution fusion | flops 6457131008 | bytes 13631488 | tf_op jit(solution)/shard_map/dot_general | solution.py:121
  310.3 11.6 %fusion.7 = bf16[1024,1536]{1,0:T(8,128)(2,1)} fusion(bf16[2048,1024]{1,0:T(8,128)(2,1)} %all-gather.7.cloned.1.call-done, bf16[2048,768]{1,0:T(8,128)(2,1)} %get-tuple-element.85, bf16[2048,768]{1,0:T(8,128)(2,1)} %get-tuple-element.84), kind=kOutput, calls=%fused_computation.25 | convolution fusion | flops 6456606720 | bytes 13631488 | tf_op jit(solution)/shard_map/dot_general | solution.py:130
  334.5 8.3 %fusion.13 = bf16[768,1024]{1,0:T(8,128)(2,1)} fusion(bf16[2048,768]{1,0:T(8,128)(2,1)} %copy-done.11, bf16[2048,1024]{1,0:T(8,128)(2,1)} %all-gather.9.cloned.1.call-done, f32[2048]{0:T(1024)S(1)} %bitcast.72), kind=kOutput, calls=%fused_computation.37 | convolution fusion | flops 3228303360 | bytes 8921088 | tf_op jit(solution)/shard_map/dot_general | solution.py:141
  342.8 21.7 %all-to-all-done.9 = bf16[16,32,1536]{2,1,0:T(8,128)(2,1)S(1)} async-done(((bf16[16,32,1536]{2,1,0:T(8,128)(2,1)}), bf16[16,32,1536]{2,1,0:T(8,128)(2,1)S(1)}, u32[]{:S(2)}, u32[]{:S(2)}) %all-to-all-start.9) | async-done | bytes 1572896 | tf_op jit(solution)/shard_map/all_to_all | solution.py:32
  365.2 9.1 %all-to-all-start.10 = ((bf16[16,32,1536]{2,1,0:T(8,128)(2,1)}), bf16[16,32,1536]{2,1,0:T(8,128)(2,1)S(1)}, u32[]{:S(2)}, u32[]{:S(2)}) async-start(bf16[16,32,1536]{2,1,0:T(8,128)(2,1)} %gather_fusion.2), calls=%async_computation.13 | async-start | bytes 3145728 | tf_op jit(solution)/shard_map/all_to_all | solution.py:32
  377.7 28.5 %all-to-all-done.10 = bf16[16,32,1536]{2,1,0:T(8,128)(2,1)S(1)} async-done(((bf16[16,32,1536]{2,1,0:T(8,128)(2,1)}), bf16[16,32,1536]{2,1,0:T(8,128)(2,1)S(1)}, u32[]{:S(2)}, u32[]{:S(2)}) %all-to-all-start.10) | async-done | bytes 1572896 | tf_op jit(solution)/shard_map/all_to_all | solution.py:32
  406.2 9.2 %all-to-all-start.11 = ((bf16[16,24,1024]{2,1,0:T(8,128)(2,1)}), bf16[16,24,1024]{2,1,0:T(8,128)(2,1)}, u32[]{:S(2)}, u32[]{:S(2)}) async-start(bf16[16,24,1024]{2,1,0:T(8,128)(2,1)} %gather_fusion.4), calls=%async_computation.14 | async-start | bytes 1572864 | tf_op jit(solution)/shard_map/all_to_all | solution.py:32
  420.2 14.0 %all-to-all-done.11 = bf16[16,24,1024]{2,1,0:T(8,128)(2,1)} async-done(((bf16[16,24,1024]{2,1,0:T(8,128)(2,1)}), bf16[16,24,1024]{2,1,0:T(8,128)(2,1)}, u32[]{:S(2)}, u32[]{:S(2)}) %all-to-all-start.11) | async-done | bytes 786464 | tf_op jit(solution)/shard_map/all_to_all | solution.py:32
  443.0 8.4 %fusion.10 = (bf16[1,512,1536]{2,1,0:T(8,128)(2,1)}, f32[512,1536]{1,0:T(8,128)}, f32[512,1536]{1,0:T(8,128)}) fusion(bf16[1,512,1536]{2,1,0:T(8,128)(2,1)S(1)} %bitcast.57, bf16[512,1536]{1,0:T(8,128)(2,1)} %reduce-scatter.9.cloned.1.call-done, f32[16,32,1536]{2,1,0:T(8,128)} %convert_multiply_fusion.3, f32[16,32,1536]{2,1,0:T(8,128)} %convert_multiply_fusion.2), kind=kLoop, calls=%fused_computation.28 | loop fusion | flops 12582912 | bytes 17301504 | tf_op jit(solution)/shard_map/convert_element_type | solution.py:25
  452.9 13.2 %all-to-all-done.12 = bf16[16,24,1024]{2,1,0:T(8,128)(2,1)S(1)} async-done(((bf16[16,24,1024]{2,1,0:T(8,128)(2,1)}), bf16[16,24,1024]{2,1,0:T(8,128)(2,1)S(1)}, u32[]{:S(2)}, u32[]{:S(2)}) %all-to-all-start.12) | async-done | bytes 786464 | tf_op jit(solution)/shard_map/all_to_all | solution.py:32
  472.0 16.9 %reduce-scatter.5.cloned.1.call-done = bf16[128,1024]{1,0:T(8,128)(2,1)} async-done(((bf16[2048,1024]{1,0:T(8,128)(2,1)}), bf16[128,1024]{1,0:T(8,128)(2,1)}) %reduce-scatter.5.cloned.1.call-update) | async-done | bytes 262160 | tf_op jit(solution)/shard_map/reduce_scatter | solution.py:119
  489.0 76.3 %reduce-scatter.7.cloned.1.call-done = bf16[128,1024]{1,0:T(8,128)(2,1)} async-done(((bf16[2048,1024]{1,0:T(8,128)(2,1)}), bf16[128,1024]{1,0:T(8,128)(2,1)}) %reduce-scatter.7.cloned.1.call-update) | async-done | bytes 262160 | tf_op jit(solution)/shard_map/reduce_scatter | solution.py:128
  (74 shorter events, 96.7 us)
Async XLA Ops:
  7.2 80.9 %copy-start.9 = (s32[16]{0:T(128)S(1)}, s32[16]{0:T(128)}, u32[]{:S(2)}) copy-start(s32[16]{0:T(128)} %param.15) | copy-start | bytes 196
  7.2 159.9 %all-gather.7.cloned.1.call-start = ((), (), s32[]{:S(2)}) async-start(), calls=%async_computation.17 | async-start | bytes 4456448 | tf_op jit(solution)/shard_map/all_gather | solution.py:76
  7.9 159.2 %all-gather.9.cloned.1.call-start = ((), (), s32[]{:S(2)}) async-start(), calls=%async_computation.18 | async-start | bytes 4456448 | tf_op jit(solution)/shard_map/all_gather | solution.py:77
  83.2 31.8 %all-to-all-start.2 = ((bf16[16,24,1024]{2,1,0:T(8,128)(2,1)}), bf16[16,24,1024]{2,1,0:T(8,128)(2,1)S(1)}, u32[]{:S(2)}, u32[]{:S(2)}) async-start(bf16[16,24,1024]{2,1,0:T(8,128)(2,1)} %bitcast.3), calls=%async_computation.2 | async-start | bytes 1572864 | tf_op jit(solution)/shard_map/all_to_all | solution.py:32
  115.0 52.1 %all-to-all-start.3 = ((bf16[16,32,1536]{2,1,0:T(8,128)(2,1)}), bf16[16,32,1536]{2,1,0:T(8,128)(2,1)S(1)}, u32[]{:S(2)}, u32[]{:S(2)}) async-start(bf16[16,32,1536]{2,1,0:T(8,128)(2,1)} %gather_fusion), calls=%async_computation.3 | async-start | bytes 3145728 | tf_op jit(solution)/shard_map/all_to_all | solution.py:32
  120.5 97.1 %all-gather.11.cloned.1.call-start = ((), (), s32[]{:S(2)}) async-start(), calls=%async_computation.23 | async-start | bytes 4718592 | tf_op jit(solution)/shard_map/all_gather | solution.py:88
  168.3 27.5 %all-to-all-start.4 = ((bf16[16,24,1024]{2,1,0:T(8,128)(2,1)}), bf16[16,24,1024]{2,1,0:T(8,128)(2,1)S(1)}, u32[]{:S(2)}, u32[]{:S(2)}) async-start(bf16[16,24,1024]{2,1,0:T(8,128)(2,1)} %gather_fusion.1), calls=%async_computation.4 | async-start | bytes 1572864 | tf_op jit(solution)/shard_map/all_to_all | solution.py:32
  195.8 37.2 %all-to-all-start.5 = ((bf16[16,32,1536]{2,1,0:T(8,128)(2,1)}), bf16[16,32,1536]{2,1,0:T(8,128)(2,1)S(1)}, u32[]{:S(2)}, u32[]{:S(2)}) async-start(bf16[16,32,1536]{2,1,0:T(8,128)(2,1)} %bitcast.60), calls=%async_computation.5 | async-start | bytes 3145728 | tf_op jit(solution)/shard_map/all_to_all | solution.py:32
  201.2 45.7 %all-gather.13.cloned.1.call-start = ((), (), s32[]{:S(2)}) async-start(), calls=%async_computation.24 | async-start | bytes 2359296 | tf_op jit(solution)/shard_map/all_gather | solution.py:90
  234.2 41.0 %all-to-all-start.6 = ((bf16[16,32,1536]{2,1,0:T(8,128)(2,1)}), bf16[16,32,1536]{2,1,0:T(8,128)(2,1)S(1)}, u32[]{:S(2)}, u32[]{:S(2)}) async-start(bf16[16,32,1536]{2,1,0:T(8,128)(2,1)} %bitcast.1), calls=%async_computation.6 | async-start | bytes 3145728 | tf_op jit(solution)/shard_map/all_to_all | solution.py:32
  246.8 14.4 %copy-start.10 = (bf16[1,768,1024]{2,1,0:T(8,128)(2,1)S(1)}, bf16[1,768,1024]{2,1,0:T(8,128)(2,1)}, u32[]{:S(2)}) copy-start(bf16[1,768,1024]{2,1,0:T(8,128)(2,1)} %all-gather.13.cloned.1.call-done) | copy-start | bytes 4718596
  275.1 27.9 %all-to-all-start.7 = ((bf16[16,24,1024]{2,1,0:T(8,128)(2,1)}), bf16[16,24,1024]{2,1,0:T(8,128)(2,1)}, u32[]{:S(2)}, u32[]{:S(2)}) async-start(bf16[16,24,1024]{2,1,0:T(8,128)(2,1)} %bitcast), calls=%async_computation.8 | async-start | bytes 1572864 | tf_op jit(solution)/shard_map/all_to_all | solution.py:32
  284.3 24.2 %copy-start.5 = (bf16[16,32,1536]{2,1,0:T(8,128)(2,1)S(1)}, bf16[16,32,1536]{2,1,0:T(8,128)(2,1)}, u32[]{:S(2)}) copy-start(bf16[16,32,1536]{2,1,0:T(8,128)(2,1)} %copy-done.4) | copy-start | bytes 4718596
  303.0 24.2 %all-to-all-start.8 = ((bf16[16,24,1024]{2,1,0:T(8,128)(2,1)}), bf16[16,24,1024]{2,1,0:T(8,128)(2,1)}, u32[]{:S(2)}, u32[]{:S(2)}) async-start(bf16[16,24,1024]{2,1,0:T(8,128)(2,1)} %bitcast.61), calls=%async_computation.10 | async-start | bytes 1572864 | tf_op jit(solution)/shard_map/all_to_all | solution.py:32
  308.5 134.6 %reduce-scatter.9.cloned.1.call-start = ((), (), s32[]{:S(2)}) async-start(), calls=%async_computation.21 | async-start | bytes 4718592 | tf_op jit(solution)/shard_map/reduce_scatter | solution.py:138
  327.2 37.2 %all-to-all-start.9 = ((bf16[16,32,1536]{2,1,0:T(8,128)(2,1)}), bf16[16,32,1536]{2,1,0:T(8,128)(2,1)S(1)}, u32[]{:S(2)}, u32[]{:S(2)}) async-start(bf16[16,32,1536]{2,1,0:T(8,128)(2,1)} %gather_fusion.3), calls=%async_computation.11 | async-start | bytes 3145728 | tf_op jit(solution)/shard_map/all_to_all | solution.py:32
  332.6 134.8 %reduce-scatter.11.cloned.1.call-start = ((), (), s32[]{:S(2)}) async-start(), calls=%async_computation.22 | async-start | bytes 2359296 | tf_op jit(solution)/shard_map/reduce_scatter | solution.py:147
  364.5 124.5 %reduce-scatter.5.cloned.1.call-start = ((), (), s32[]{:S(2)}) async-start(), calls=%async_computation.19 | async-start | bytes 4456448 | tf_op jit(solution)/shard_map/reduce_scatter | solution.py:119
  365.2 41.0 %all-to-all-start.10 = ((bf16[16,32,1536]{2,1,0:T(8,128)(2,1)}), bf16[16,32,1536]{2,1,0:T(8,128)(2,1)S(1)}, u32[]{:S(2)}, u32[]{:S(2)}) async-start(bf16[16,32,1536]{2,1,0:T(8,128)(2,1)} %gather_fusion.2), calls=%async_computation.13 | async-start | bytes 3145728 | tf_op jit(solution)/shard_map/all_to_all | solution.py:32
  374.4 190.9 %reduce-scatter.7.cloned.1.call-start = ((), (), s32[]{:S(2)}) async-start(), calls=%async_computation.20 | async-start | bytes 4456448 | tf_op jit(solution)/shard_map/reduce_scatter | solution.py:128
  406.2 27.9 %all-to-all-start.11 = ((bf16[16,24,1024]{2,1,0:T(8,128)(2,1)}), bf16[16,24,1024]{2,1,0:T(8,128)(2,1)}, u32[]{:S(2)}, u32[]{:S(2)}) async-start(bf16[16,24,1024]{2,1,0:T(8,128)(2,1)} %gather_fusion.4), calls=%async_computation.14 | async-start | bytes 1572864 | tf_op jit(solution)/shard_map/all_to_all | solution.py:32
  420.2 22.9 %copy-start.1 = (bf16[16,32,1536]{2,1,0:T(8,128)(2,1)S(1)}, bf16[16,32,1536]{2,1,0:T(8,128)(2,1)}, u32[]{:S(2)}) copy-start(bf16[16,32,1536]{2,1,0:T(8,128)(2,1)} %copy-done) | copy-start | bytes 4718596
  434.1 31.9 %all-to-all-start.12 = ((bf16[16,24,1024]{2,1,0:T(8,128)(2,1)}), bf16[16,24,1024]{2,1,0:T(8,128)(2,1)S(1)}, u32[]{:S(2)}, u32[]{:S(2)}) async-start(bf16[16,24,1024]{2,1,0:T(8,128)(2,1)} %gather_fusion.5), calls=%async_computation.16 | async-start | bytes 1572864 | tf_op jit(solution)/shard_map/all_to_all | solution.py:32
  451.5 15.9 %copy-start.3 = (bf16[16,24,1024]{2,1,0:T(8,128)(2,1)S(1)}, bf16[16,24,1024]{2,1,0:T(8,128)(2,1)}, u32[]{:S(2)}) copy-start(bf16[16,24,1024]{2,1,0:T(8,128)(2,1)} %copy-done.2) | copy-start | bytes 2359300
  (7 other events, 39.4 us)
Sparse Core Ops, SparseCore 0:
  10.1 71.8 all-gather.6
  84.2 80.1 all-gather.8
  168.4 49.2 all-gather.10
  219.6 27.1 all-gather.12
  327.3 44.3 reduce-scatter.8
  373.8 26.1 reduce-scatter.10
  404.4 84.4 reduce-scatter.4
  493.4 71.8 reduce-scatter.6

commit v3 on v2

--- a/solution.py
+++ b/solution.py
@@ -70,14 +70,14 @@
     own_gates = gate_weights.reshape(row_count, top_count)
     hits = own_routes[None, :, :] == expert_plan[:, None, None]
     sent_gates = jnp.sum(jnp.where(hits, own_gates[None, :, :], 0.0), axis=2)
-    gate_column = lax.all_to_all(
-        sent_gates, "expert", split_axis=0, concat_axis=0, tiled=True
+    all_gates = lax.all_gather(sent_gates, "expert", axis=0, tiled=False)
+    gate_column = lax.dynamic_index_in_dim(
+        all_gates, lax.axis_index("expert"), axis=1, keepdims=False
     ).reshape(count * row_count, 1)
     rows = lax.all_gather(tokens.reshape(row_count, width), "expert", axis=0, tiled=True)
     upstream = lax.all_gather(cotangent.reshape(row_count, width), "expert", axis=0, tiled=True)
 
-    pieces, gate_column = tie(cut(weight_in, count), gate_column)
-    spread_in = exchange(pieces)
+    spread_in = exchange(cut(weight_in, count))
     pieces, spread_in = tie(cut(weight_out, count), spread_in)
     spread_out = exchange(pieces)
     pieces, spread_out = tie(pick(spread_in, expert_plan), spread_out)
@@ -135,6 +135,7 @@
         pick(spread_one, expert_plan), spread_four, grad_in, upstream
     )
     landed_one = exchange(pieces)
+    grad_in, layer_rows = tie(grad_in, layer_rows)
     share_in = lax.psum_scatter(grad_in, "dp", scatter_dimension=0, tiled=True)
     scaled = (gate_column * late_upstream.astype(jnp.float32)).astype(jnp.bfloat16)
     grad_out = row_major(
@@ -142,12 +143,16 @@
             hidden, scaled, (((0,), (0,)), ((), ())), preferred_element_type=jnp.float32
         ).astype(jnp.bfloat16)
     )
-    pieces, landed_one, grad_out = tie(pick(spread_two, expert_plan), landed_one, grad_out)
+    pieces, landed_one, grad_out, layer_rows = tie(
+        pick(spread_two, expert_plan), landed_one, grad_out, layer_rows
+    )
     landed_two = exchange(pieces)
     share_out = lax.psum_scatter(grad_out, "dp", scatter_dimension=0, tiled=True)
     pieces, landed_two = tie(pick(spread_three, expert_plan), landed_two)
     landed_three = exchange(pieces)
-    pieces, landed_three = tie(pick(spread_four, expert_plan), landed_three)
+    pieces, landed_three, token_rows = tie(
+        pick(spread_four, expert_plan), landed_three, token_rows
+    )
     landed_four = exchange(pieces)
 
     new_in, first_in_new, second_in_new = adam_update(

time: 574 us -> 593 us (1.033)
  blocking collectives: 72.2 us -> 107 us
  waiting for transfers between devices: 297 us -> 269 us
  starting transfers between devices: 77.7 us -> 90 us
    reduce_scatter x1, waiting for transfers between devices: 76.3 us -> 19.8 us  [on_device(): lax.psum_scatter(token_part, 'expert', scatter_dimension=0, tiled=True)]
    all_gather x0 -> x1, blocking collectives: none -> 42.4 us  [on_device(): all_gates = lax.all_gather(sent_gates, 'expert', axis=0, tiled=False)]
    reduce_scatter x1, waiting for transfers between devices: 0.01 us -> 40.2 us  [on_device(): share_in = lax.psum_scatter(grad_in, 'dp', scatter_dimension=0, tiled=True)]
    all_to_all x1 -> x0, blocking collectives: 13.6 us -> none  [on_device(): lax.all_to_all(sent_gates, 'expert', split_axis=0, concat_axis=0, tiled=T...]
    all_to_all x11, starting transfers between devices: 77.3 us -> 89.5 us  [exchange(): lax.all_to_all(pieces, 'expert', split_axis=0, concat_axis=0, tiled=True)]
    all_to_all x1, blocking collectives: 58.6 us -> 64.9 us  [exchange(): lax.all_to_all(pieces, 'expert', split_axis=0, concat_axis=0, tiled=True)]
    all_to_all x11, waiting for transfers between devices: 187 us -> 181 us  [exchange(): lax.all_to_all(pieces, 'expert', split_axis=0, concat_axis=0, tiled=True)]
  transfers between devices with their start and end apart: 19 -> 19, of which waited for: 15 -> 14; matrix products, arithmetic and copies ran while one was open for 19% -> 17% of each run, Pallas kernels for 0% -> 0%
where the time goes in v3:
time: 593 us; the launch traced here: 592 us
  waiting for transfers between devices  269 us (45%)
  blocking collectives  107 us (18%)
  starting transfers between devices  90 us (15%)
  matrix products  61.7 us (10%)
  other arithmetic  34.5 us (6%)
  local copies, waits for them, and re-layouts  15.1 us (3%)
  between operations  14.3 us (2%)
    all_to_all x11, waiting for transfers between devices, exchange(): lax.all_to_all(pieces, 'expert', split_axis=0, concat_axis=0, tiled=True)  181 us
    all_to_all x11, starting transfers between devices, exchange(): lax.all_to_all(pieces, 'expert', split_axis=0, concat_axis=0, tiled=True)  89.5 us
    all_to_all x1, blocking collectives, exchange(): lax.all_to_all(pieces, 'expert', split_axis=0, concat_axis=0, tiled=True)  64.9 us
    all_gather x1, blocking collectives, on_device(): all_gates = lax.all_gather(sent_gates, 'expert', axis=0, tiled=False)  42.4 us
    reduce_scatter x1, waiting for transfers between devices, on_device(): share_in = lax.psum_scatter(grad_in, 'dp', scatter_dimension=0, tiled=True)  40.2 us
    reduce_scatter x1, waiting for transfers between devices, on_device(): lax.psum_scatter(token_part, 'expert', scatter_dimension=0, tiled=True)  19.8 us
    reduce_scatter x1, waiting for transfers between devices, on_device(): lax.psum_scatter(weighted, 'expert', scatter_dimension=0, tiled=True)  15.6 us
    convert_element_type x2, other arithmetic, adam_update(): (master - learn_rate * (ratio + decay_rate * master)).astype(jnp.bfloat16)  13.6 us
  transfers between devices with their start and end apart: 19, of which 14 were waited for; matrix products, arithmetic and copies ran while one was open for 17% of the time, Pallas kernels for 0%

profile of v3, /device:TPU:0, one launch (start us, length us, event | category | flops | bytes accessed | tf_op | source)
XLA Modules:
  0.0 592.0 jit_solution(4507128820886234461)
XLA Ops:
  8.7 64.9 %all_to_all.60 = bf16[16,32,1536]{2,1,0:T(8,128)(2,1)S(1)} all-to-all(bf16[16,32,1536]{2,1,0:T(8,128)(2,1)} %bitcast.63), channel_id=1, replica_groups=mesh['expert'=16,'dp'=2] {'expert'}, dimensions={0} | all-to-all | bytes 3145728 | tf_op jit(solution)/shard_map/all_to_all | solution.py:32
  73.5 8.8 %all-to-all-start.1 = ((bf16[16,24,1024]{2,1,0:T(8,128)(2,1)}), bf16[16,24,1024]{2,1,0:T(8,128)(2,1)S(1)}, u32[]{:S(2)}, u32[]{:S(2)}) async-start(bf16[16,24,1024]{2,1,0:T(8,128)(2,1)} %bitcast.3), calls=%async_computation.1 | async-start | bytes 1572864 | tf_op jit(solution)/shard_map/all_to_all | solution.py:32
  84.1 22.5 %all-to-all-done.1 = bf16[16,24,1024]{2,1,0:T(8,128)(2,1)S(1)} async-done(((bf16[16,24,1024]{2,1,0:T(8,128)(2,1)}), bf16[16,24,1024]{2,1,0:T(8,128)(2,1)S(1)}, u32[]{:S(2)}, u32[]{:S(2)}) %all-to-all-start.1) | async-done | bytes 786464 | tf_op jit(solution)/shard_map/all_to_all | solution.py:32
  116.3 46.4 %all-to-all-done.2 = bf16[16,32,1536]{2,1,0:T(8,128)(2,1)S(1)} async-done(((bf16[16,32,1536]{2,1,0:T(8,128)(2,1)}), bf16[16,32,1536]{2,1,0:T(8,128)(2,1)S(1)}, u32[]{:S(2)}, u32[]{:S(2)}) %all-to-all-start.2) | async-done | bytes 1572896 | tf_op jit(solution)/shard_map/all_to_all | solution.py:32
  164.0 8.8 %all-to-all-start.3 = ((bf16[16,24,1024]{2,1,0:T(8,128)(2,1)}), bf16[16,24,1024]{2,1,0:T(8,128)(2,1)S(1)}, u32[]{:S(2)}, u32[]{:S(2)}) async-start(bf16[16,24,1024]{2,1,0:T(8,128)(2,1)} %gather_fusion.1), calls=%async_computation.3 | async-start | bytes 1572864 | tf_op jit(solution)/shard_map/all_to_all | solution.py:32
  176.1 15.3 %all-to-all-done.3 = bf16[16,24,1024]{2,1,0:T(8,128)(2,1)S(1)} async-done(((bf16[16,24,1024]{2,1,0:T(8,128)(2,1)}), bf16[16,24,1024]{2,1,0:T(8,128)(2,1)S(1)}, u32[]{:S(2)}, u32[]{:S(2)}) %all-to-all-start.3) | async-done | bytes 786464 | tf_op jit(solution)/shard_map/all_to_all | solution.py:32
  202.8 10.5 %all-gather.12.cloned.1.call-done = bf16[1,1024,1536]{2,1,0:T(8,128)(2,1)} async-done(((bf16[1,512,1536]{2,1,0:T(8,128)(2,1)}), bf16[1,1024,1536]{2,1,0:T(8,128)(2,1)}) %all-gather.12.cloned.1.call-update) | async-done | bytes 3145744 | tf_op jit(solution)/shard_map/all_gather | solution.py:88
  213.3 12.3 %fusion.23 = f32[2048,1536]{1,0:T(8,128)} fusion(bf16[2048,1024]{1,0:T(8,128)(2,1)} %all-gather.8.cloned.1.call-done, bf16[1,1024,1536]{2,1,0:T(8,128)(2,1)} %all-gather.12.cloned.1.call-done), kind=kOutput, calls=%fused_computation.52 | convolution fusion | flops 6442450944 | bytes 19922944 | tf_op jit(solution)/shard_map/dot_general | solution.py:94
  228.7 9.1 %all-to-all-start.5 = ((bf16[16,32,1536]{2,1,0:T(8,128)(2,1)}), bf16[16,32,1536]{2,1,0:T(8,128)(2,1)S(1)}, u32[]{:S(2)}, u32[]{:S(2)}) async-start(bf16[16,32,1536]{2,1,0:T(8,128)(2,1)} %bitcast.57), calls=%async_computation.5 | async-start | bytes 3145728 | tf_op jit(solution)/shard_map/all_to_all | solution.py:32
  237.9 42.4 %all-gather.1 = f32[256,128]{1,0:T(8,128)S(1)} all-gather(f32[16,128]{1,0:T(8,128)S(1)} %select_reduce_fusion), channel_id=3, replica_groups=mesh['expert'=16,'dp'=2] {'expert'}, dimensions={0}, use_global_device_ids=true | all-gather | bytes 139264 | tf_op jit(solution)/shard_map/all_gather | solution.py:73
  280.4 12.8 %multiply_convert_fusion.4 = (bf16[2048,768]{1,0:T(8,128)(2,1)}, bf16[2048,768]{1,0:T(8,128)(2,1)}, bf16[2048,768]{1,0:T(8,128)(2,1)S(1)}) fusion(f32[2048,1536]{1,0:T(8,128)} %fusion.23, bf16[1,768,1024]{2,1,0:T(8,128)(2,1)} %all-gather.14.cloned.1.call-done, bf16[2048,1024]{1,0:T(8,128)(2,1)} %all-gather.10.cloned.1.call-done, f32[2048]{0:T(1024)S(1)} %bitcast.69), kind=kOutput, calls=%fused_computation.11 | convolution fusion | flops 3252682752 | bytes 27795456 | tf_op jit(solution)/shard_map/dot_general | solution.py:103
  302.3 8.5 %all-to-all-start.6 = ((bf16[16,24,1024]{2,1,0:T(8,128)(2,1)}), bf16[16,24,1024]{2,1,0:T(8,128)(2,1)}, u32[]{:S(2)}, u32[]{:S(2)}) async-start(bf16[16,24,1024]{2,1,0:T(8,128)(2,1)} %bitcast.59), calls=%async_computation.6 | async-start | bytes 1572864 | tf_op jit(solution)/shard_map/all_to_all | solution.py:32
  311.0 12.1 %fusion.6 = bf16[2048,1024]{1,0:T(8,128)(2,1)} fusion(bf16[1024,1536]{1,0:T(8,128)(2,1)} %bitcast.72, bf16[2048,768]{1,0:T(8,128)(2,1)} %get-tuple-element.89, bf16[2048,768]{1,0:T(8,128)(2,1)} %get-tuple-element.88), kind=kOutput, calls=%fused_computation.24 | convolution fusion | flops 6457131008 | bytes 13631488 | tf_op jit(solution)/shard_map/dot_general | solution.py:121
  336.9 11.6 %fusion.7 = bf16[1024,1536]{1,0:T(8,128)(2,1)} fusion(bf16[2048,1024]{1,0:T(8,128)(2,1)} %all-gather.8.cloned.1.call-done, bf16[2048,768]{1,0:T(8,128)(2,1)} %get-tuple-element.89, bf16[2048,768]{1,0:T(8,128)(2,1)} %get-tuple-element.88), kind=kOutput, calls=%fused_computation.25 | convolution fusion | flops 6456606720 | bytes 13631488 | tf_op jit(solution)/shard_map/dot_general | solution.py:130
  348.4 16.2 %all-to-all-done.7 = bf16[16,24,1024]{2,1,0:T(8,128)(2,1)} async-done(((bf16[16,24,1024]{2,1,0:T(8,128)(2,1)}), bf16[16,24,1024]{2,1,0:T(8,128)(2,1)}, u32[]{:S(2)}, u32[]{:S(2)}) %all-to-all-start.7) | async-done | bytes 786464 | tf_op jit(solution)/shard_map/all_to_all | solution.py:32
  364.6 8.9 %all-to-all-start.8 = ((bf16[16,32,1536]{2,1,0:T(8,128)(2,1)}), bf16[16,32,1536]{2,1,0:T(8,128)(2,1)S(1)}, u32[]{:S(2)}, u32[]{:S(2)}) async-start(bf16[16,32,1536]{2,1,0:T(8,128)(2,1)} %gather_fusion.3), calls=%async_computation.8 | async-start | bytes 3145728 | tf_op jit(solution)/shard_map/all_to_all | solution.py:32
  383.2 15.6 %reduce-scatter.5.cloned.1.call-done = bf16[128,1024]{1,0:T(8,128)(2,1)} async-done(((bf16[2048,1024]{1,0:T(8,128)(2,1)}), bf16[128,1024]{1,0:T(8,128)(2,1)}) %reduce-scatter.5.cloned.1.call-update) | async-done | bytes 262160 | tf_op jit(solution)/shard_map/reduce_scatter | solution.py:119
  398.8 14.5 %all-to-all-done.8 = bf16[16,32,1536]{2,1,0:T(8,128)(2,1)S(1)} async-done(((bf16[16,32,1536]{2,1,0:T(8,128)(2,1)}), bf16[16,32,1536]{2,1,0:T(8,128)(2,1)S(1)}, u32[]{:S(2)}, u32[]{:S(2)}) %all-to-all-start.8) | async-done | bytes 1572896 | tf_op jit(solution)/shard_map/all_to_all | solution.py:32
  413.4 9.0 %all-to-all-start.9 = ((bf16[16,32,1536]{2,1,0:T(8,128)(2,1)}), bf16[16,32,1536]{2,1,0:T(8,128)(2,1)S(1)}, u32[]{:S(2)}, u32[]{:S(2)}) async-start(bf16[16,32,1536]{2,1,0:T(8,128)(2,1)} %gather_fusion.2), calls=%async_computation.10 | async-start | bytes 3145728 | tf_op jit(solution)/shard_map/all_to_all | solution.py:32
  425.8 42.5 %all-to-all-done.9 = bf16[16,32,1536]{2,1,0:T(8,128)(2,1)S(1)} async-done(((bf16[16,32,1536]{2,1,0:T(8,128)(2,1)}), bf16[16,32,1536]{2,1,0:T(8,128)(2,1)S(1)}, u32[]{:S(2)}, u32[]{:S(2)}) %all-to-all-start.9) | async-done | bytes 1572896 | tf_op jit(solution)/shard_map/all_to_all | solution.py:32
  468.3 11.9 %all-to-all-start.10 = ((bf16[16,24,1024]{2,1,0:T(8,128)(2,1)}), bf16[16,24,1024]{2,1,0:T(8,128)(2,1)}, u32[]{:S(2)}, u32[]{:S(2)}) async-start(bf16[16,24,1024]{2,1,0:T(8,128)(2,1)} %gather_fusion.5), calls=%async_computation.11 | async-start | bytes 1572864 | tf_op jit(solution)/shard_map/all_to_all | solution.py:32
  482.8 19.8 %reduce-scatter.7.cloned.1.call-done = bf16[128,1024]{1,0:T(8,128)(2,1)} async-done(((bf16[2048,1024]{1,0:T(8,128)(2,1)}), bf16[128,1024]{1,0:T(8,128)(2,1)}) %reduce-scatter.7.cloned.1.call-update) | async-done | bytes 262160 | tf_op jit(solution)/shard_map/reduce_scatter | solution.py:128
  516.9 12.0 %all-to-all-done.11 = bf16[16,24,1024]{2,1,0:T(8,128)(2,1)} async-done(((bf16[16,24,1024]{2,1,0:T(8,128)(2,1)}), bf16[16,24,1024]{2,1,0:T(8,128)(2,1)}, u32[]{:S(2)}, u32[]{:S(2)}) %all-to-all-start.11) | async-done | bytes 786464 | tf_op jit(solution)/shard_map/all_to_all | solution.py:32
  536.5 40.2 %reduce-scatter.9.cloned.1.call-done = bf16[512,1536]{1,0:T(8,128)(2,1)} async-done(((bf16[1024,1536]{1,0:T(8,128)(2,1)}), bf16[512,1536]{1,0:T(8,128)(2,1)}) %reduce-scatter.9.cloned.1.call-update) | async-done | bytes 1572880 | tf_op jit(solution)/shard_map/reduce_scatter | solution.py:139
  (69 shorter events, 101.1 us)
Async XLA Ops:
  7.2 75.2 %copy-start.6 = (s32[16]{0:T(128)S(1)}, s32[16]{0:T(128)}, u32[]{:S(2)}) copy-start(s32[16]{0:T(128)} %param.15) | copy-start | bytes 196
  7.2 155.6 %all-gather.10.cloned.1.call-start = ((), (), s32[]{:S(2)}) async-start(), calls=%async_computation.17 | async-start | bytes 4456448 | tf_op jit(solution)/shard_map/all_gather | solution.py:78
  7.9 154.9 %all-gather.8.cloned.1.call-start = ((), (), s32[]{:S(2)}) async-start(), calls=%async_computation.16 | async-start | bytes 4456448 | tf_op jit(solution)/shard_map/all_gather | solution.py:77
  73.5 33.2 %all-to-all-start.1 = ((bf16[16,24,1024]{2,1,0:T(8,128)(2,1)}), bf16[16,24,1024]{2,1,0:T(8,128)(2,1)S(1)}, u32[]{:S(2)}, u32[]{:S(2)}) async-start(bf16[16,24,1024]{2,1,0:T(8,128)(2,1)} %bitcast.3), calls=%async_computation.1 | async-start | bytes 1572864 | tf_op jit(solution)/shard_map/all_to_all | solution.py:32
  106.7 56.1 %all-to-all-start.2 = ((bf16[16,32,1536]{2,1,0:T(8,128)(2,1)}), bf16[16,32,1536]{2,1,0:T(8,128)(2,1)S(1)}, u32[]{:S(2)}, u32[]{:S(2)}) async-start(bf16[16,32,1536]{2,1,0:T(8,128)(2,1)} %gather_fusion), calls=%async_computation.2 | async-start | bytes 3145728 | tf_op jit(solution)/shard_map/all_to_all | solution.py:32
  114.8 98.5 %all-gather.12.cloned.1.call-start = ((), (), s32[]{:S(2)}) async-start(), calls=%async_computation.22 | async-start | bytes 4718592 | tf_op jit(solution)/shard_map/all_gather | solution.py:88
  164.0 27.5 %all-to-all-start.3 = ((bf16[16,24,1024]{2,1,0:T(8,128)(2,1)}), bf16[16,24,1024]{2,1,0:T(8,128)(2,1)S(1)}, u32[]{:S(2)}, u32[]{:S(2)}) async-start(bf16[16,24,1024]{2,1,0:T(8,128)(2,1)} %gather_fusion.1), calls=%async_computation.3 | async-start | bytes 1572864 | tf_op jit(solution)/shard_map/all_to_all | solution.py:32
  191.4 8.7 %copy-start.2 = (bf16[16,24,1024]{2,1,0:T(8,128)(2,1)}, bf16[16,24,1024]{2,1,0:T(8,128)(2,1)S(1)}, u32[]{:S(2)}) copy-start(bf16[16,24,1024]{2,1,0:T(8,128)(2,1)S(1)} %all-to-all-done.3) | copy-start | bytes 2359300
  191.4 37.2 %all-to-all-start.4 = ((bf16[16,32,1536]{2,1,0:T(8,128)(2,1)}), bf16[16,32,1536]{2,1,0:T(8,128)(2,1)S(1)}, u32[]{:S(2)}, u32[]{:S(2)}) async-start(bf16[16,32,1536]{2,1,0:T(8,128)(2,1)} %bitcast.58), calls=%async_computation.4 | async-start | bytes 3145728 | tf_op jit(solution)/shard_map/all_to_all | solution.py:32
  196.8 83.5 %all-gather.14.cloned.1.call-start = ((), (), s32[]{:S(2)}) async-start(), calls=%async_computation.23 | async-start | bytes 2359296 | tf_op jit(solution)/shard_map/all_gather | solution.py:90
  228.7 71.2 %all-to-all-start.5 = ((bf16[16,32,1536]{2,1,0:T(8,128)(2,1)}), bf16[16,32,1536]{2,1,0:T(8,128)(2,1)S(1)}, u32[]{:S(2)}, u32[]{:S(2)}) async-start(bf16[16,32,1536]{2,1,0:T(8,128)(2,1)} %bitcast.57), calls=%async_computation.5 | async-start | bytes 3145728 | tf_op jit(solution)/shard_map/all_to_all | solution.py:32
  237.8 161.1 %reduce-scatter.5.cloned.1.call-start = ((), (), s32[]{:S(2)}) async-start(), calls=%async_computation.18 | async-start | bytes 4456448 | tf_op jit(solution)/shard_map/reduce_scatter | solution.py:119
  280.4 14.4 %copy-start.7 = (bf16[1,768,1024]{2,1,0:T(8,128)(2,1)S(1)}, bf16[1,768,1024]{2,1,0:T(8,128)(2,1)}, u32[]{:S(2)}) copy-start(bf16[1,768,1024]{2,1,0:T(8,128)(2,1)} %all-gather.14.cloned.1.call-done) | copy-start | bytes 4718596
  302.3 27.2 %all-to-all-start.6 = ((bf16[16,24,1024]{2,1,0:T(8,128)(2,1)}), bf16[16,24,1024]{2,1,0:T(8,128)(2,1)}, u32[]{:S(2)}, u32[]{:S(2)}) async-start(bf16[16,24,1024]{2,1,0:T(8,128)(2,1)} %bitcast.59), calls=%async_computation.6 | async-start | bytes 1572864 | tf_op jit(solution)/shard_map/all_to_all | solution.py:32
  310.7 191.9 %reduce-scatter.7.cloned.1.call-start = ((), (), s32[]{:S(2)}) async-start(), calls=%async_computation.19 | async-start | bytes 4456448 | tf_op jit(solution)/shard_map/reduce_scatter | solution.py:128
  329.5 35.1 %all-to-all-start.7 = ((bf16[16,24,1024]{2,1,0:T(8,128)(2,1)}), bf16[16,24,1024]{2,1,0:T(8,128)(2,1)}, u32[]{:S(2)}, u32[]{:S(2)}) async-start(bf16[16,24,1024]{2,1,0:T(8,128)(2,1)} %bitcast.60), calls=%async_computation.7 | async-start | bytes 1572864 | tf_op jit(solution)/shard_map/all_to_all | solution.py:32
  364.6 48.8 %all-to-all-start.8 = ((bf16[16,32,1536]{2,1,0:T(8,128)(2,1)}), bf16[16,32,1536]{2,1,0:T(8,128)(2,1)S(1)}, u32[]{:S(2)}, u32[]{:S(2)}) async-start(bf16[16,32,1536]{2,1,0:T(8,128)(2,1)} %gather_fusion.3), calls=%async_computation.8 | async-start | bytes 3145728 | tf_op jit(solution)/shard_map/all_to_all | solution.py:32
  373.5 157.9 %reduce-scatter.11.cloned.1.call-start = ((), (), s32[]{:S(2)}) async-start(), calls=%async_computation.21 | async-start | bytes 2359296 | tf_op jit(solution)/shard_map/reduce_scatter | solution.py:150
  413.4 54.9 %all-to-all-start.9 = ((bf16[16,32,1536]{2,1,0:T(8,128)(2,1)}), bf16[16,32,1536]{2,1,0:T(8,128)(2,1)S(1)}, u32[]{:S(2)}, u32[]{:S(2)}) async-start(bf16[16,32,1536]{2,1,0:T(8,128)(2,1)} %gather_fusion.2), calls=%async_computation.10 | async-start | bytes 3145728 | tf_op jit(solution)/shard_map/all_to_all | solution.py:32
  422.4 154.4 %reduce-scatter.9.cloned.1.call-start = ((), (), s32[]{:S(2)}) async-start(), calls=%async_computation.20 | async-start | bytes 4718592 | tf_op jit(solution)/shard_map/reduce_scatter | solution.py:139
  468.3 36.2 %all-to-all-start.10 = ((bf16[16,24,1024]{2,1,0:T(8,128)(2,1)}), bf16[16,24,1024]{2,1,0:T(8,128)(2,1)}, u32[]{:S(2)}, u32[]{:S(2)}) async-start(bf16[16,24,1024]{2,1,0:T(8,128)(2,1)} %gather_fusion.5), calls=%async_computation.11 | async-start | bytes 1572864 | tf_op jit(solution)/shard_map/all_to_all | solution.py:32
  504.6 24.3 %all-to-all-start.11 = ((bf16[16,24,1024]{2,1,0:T(8,128)(2,1)}), bf16[16,24,1024]{2,1,0:T(8,128)(2,1)}, u32[]{:S(2)}, u32[]{:S(2)}) async-start(bf16[16,24,1024]{2,1,0:T(8,128)(2,1)} %gather_fusion.4), calls=%async_computation.15 | async-start | bytes 1572864 | tf_op jit(solution)/shard_map/all_to_all | solution.py:32
  514.3 17.1 %copy-start.3 = (bf16[16,24,1024]{2,1,0:T(8,128)(2,1)S(1)}, bf16[16,24,1024]{2,1,0:T(8,128)(2,1)}, u32[]{:S(2)}) copy-start(bf16[16,24,1024]{2,1,0:T(8,128)(2,1)} %copy-done.2) | copy-start | bytes 2359300
  531.4 45.4 %copy-start.1 = (bf16[16,32,1536]{2,1,0:T(8,128)(2,1)S(1)}, bf16[16,32,1536]{2,1,0:T(8,128)(2,1)}, u32[]{:S(2)}) copy-start(bf16[16,32,1536]{2,1,0:T(8,128)(2,1)} %copy-done) | copy-start | bytes 4718596
  (4 other events, 9.4 us)
Sparse Core Ops, SparseCore 0:
  10.1 70.2 all-gather.9
  82.6 78.2 all-gather.7
  164.1 49.1 all-gather.11
  215.3 27.1 all-gather.13
  300.0 98.8 reduce-scatter.4
  403.1 99.4 reduce-scatter.6
  505.4 25.5 reduce-scatter.10
  533.3 43.3 reduce-scatter.8
